TPU v7x, 256 devices: a whole 4x4x8 slice. The times are simulated.
256 devices in a mesh: dp: 8 (over z), seq: 32 (over x, y, core).
Axes of the slice: x: 4, y: 4, z: 8, core: 2. Of those that a mesh axis runs over, the one named last changes fastest.
Arguments:
- query: bfloat16 [8, 8192, 1024], P('dp', 'seq'), may hold values from -150 to 150
- key: bfloat16 [8, 8192, 128], P('dp', 'seq'), may hold values from -5 to 5
- value: bfloat16 [8, 8192, 128], P('dp', 'seq'), may hold values from -6 to 6
- ssm_input: bfloat16 [8, 8192, 1024], P('dp', 'seq'), may hold values from -9 to 9
- in_b: bfloat16 [8, 8192, 128], P('dp', 'seq'), may hold values from -0.5 to 0.5
- in_c: bfloat16 [8, 8192, 128], P('dp', 'seq'), may hold values from -0.5 to 0.5
- step: float32 [8, 8192, 8], P('dp', 'seq'), may hold values from 0.3 to 24576
- rate_log: float32 [8], replicated, may hold values from -20 to 0
- skip: float32 [8], replicated, may hold values from 0.5 to 1.5
- block_mask: int32 [8, 64, 64], P('dp'), may hold values from 0 to 1, as said below
- grad_out: bfloat16 [8, 8192, 1024], P('dp', 'seq'), may hold values from -10 to 10
Outputs:
- layer_out: bfloat16 [8, 8192, 1024], P('dp', 'seq')
- query_gradient: bfloat16 [8, 8192, 1024], P('dp', 'seq')
- key_gradient: bfloat16 [8, 8192, 128], P('dp', 'seq')
- value_gradient: bfloat16 [8, 8192, 128], P('dp', 'seq')
- grad_input: bfloat16 [8, 8192, 1024], P('dp', 'seq')
- grad_in_b: bfloat16 [8, 8192, 128], P('dp', 'seq')
- grad_in_c: bfloat16 [8, 8192, 128], P('dp', 'seq')
- grad_rate_log: float32 [8], replicated
- grad_skip: float32 [8], replicated
Inputs may be any that keep to these rules, and one draw needn't show every extreme that they name: block_mask[b, i, i] = 1; every row holds at most 24 ones, and the last row of every sequence's mask holds exactly 24.
All inputs are finite; a program needn't handle non-finite values.
Results may differ from a plain program's by a relative error of at most 0.02.
Values may be sent and summed in bfloat16 or wider, within the bound.
A program may use at most 192 MiB of HBM per device.

v0:
```python
import functools

import jax
import jax.numpy as jnp
from jax import lax
from jax.experimental import pallas as pl
from jax.experimental.pallas import tpu as pltpu
from jax.sharding import PartitionSpec as P

HW = 128
HEADS = 8
BT = 128
MOST = 24
MOST_PAIRS = MOST // 2
FACTOR = HW ** (-0.5)
LOG2E = 1.4426950408889634
BF = jnp.bfloat16
F32 = jnp.float32
MESH = pl.DeviceIdType.MESH
HIGH = lax.Precision.HIGHEST

VM = pl.BlockSpec(memory_space=pltpu.VMEM)
SM = pl.BlockSpec(memory_space=pltpu.SMEM)


def nn(a, b):
    return lax.dot_general(a, b, (((1,), (0,)), ((), ())), preferred_element_type=F32)


def nt(a, b):
    return lax.dot_general(a, b, (((1,), (1,)), ((), ())), preferred_element_type=F32)


def tn(a, b):
    return lax.dot_general(a, b, (((0,), (0,)), ((), ())), preferred_element_type=F32)


def cols(h):
    return pl.ds(h * HW, HW)


def attention_kernel(
    mask_ref, q_ref, g_ref, k_ref, v_ref,
    o_ref, dq_ref, tk_ref, tv_ref,
    s_buf, acc_k, acc_v, qs, gs, g_t, o_t, dq_t, picked,
):
    total_blocks = mask_ref.shape[1]
    seq_at = lax.axis_index("seq")
    per_device = q_ref.shape[0] // BT
    acc_k[...] = jnp.zeros_like(acc_k)
    acc_v[...] = jnp.zeros_like(acc_v)

    @pl.loop(0, per_device)
    def _(block):
        row = seq_at * per_device + block

        def note(j, n):
            picked[n] = j
            return n + mask_ref[row, j]

        count = lax.fori_loop(0, total_blocks, note, jnp.int32(0))
        picked[count] = picked[0]
        pairs = (count + 1) // 2
        rows = pl.ds(pl.multiple_of(block * BT, BT), BT)
        for h in range(HEADS):
            qs[cols(h), :] = q_ref[rows, cols(h)]
            g_head = g_ref[rows, cols(h)]
            gs[cols(h), :] = g_head
            g_t[:, cols(h)] = g_head.astype(F32).T

        def starts(p):
            return tuple(pl.multiple_of(picked[2 * p + i] * BT, BT) for i in range(2))

        def pair_of(ref, p):
            first, second = starts(p)
            return jnp.concatenate([ref[pl.ds(first, BT), :], ref[pl.ds(second, BT), :]], axis=0)

        def score_step(p, top):
            s = nt(pair_of(k_ref, p), qs[...])
            bias = jnp.where(2 * p + 1 < count, 0.0, -1e30).astype(F32)
            s = jnp.concatenate([s[:BT], s[BT:] + bias], axis=0)
            s_buf[p] = s
            return jnp.maximum(top, jnp.max(s.reshape(-1, 8, s.shape[1]), axis=0))

        top = lax.fori_loop(
            0, pairs, score_step, jnp.full((8, HEADS * BT), -3e38, F32)
        )
        top = jnp.max(top, axis=0, keepdims=True)
        o_t[...] = jnp.zeros_like(o_t)

        def weight_step(p, total):
            w = jnp.exp2((s_buf[p] - top) * (FACTOR * LOG2E))
            s_buf[p] = w
            o_t[...] += nn(pair_of(v_ref, p).T, w.astype(BF))
            return total + jnp.sum(w.reshape(-1, 8, w.shape[1]), axis=0)

        total = lax.fori_loop(0, pairs, weight_step, jnp.zeros((8, HEADS * BT), F32))
        inverse = 1.0 / jnp.sum(total, axis=0, keepdims=True)
        o_t[...] = o_t[...] * inverse
        delta = jnp.sum(o_t[...] * g_t[...], axis=0, keepdims=True)
        for h in range(HEADS):
            o_ref[rows, cols(h)] = o_t[:, cols(h)].T
        dq_t[...] = jnp.zeros_like(dq_t)

        def gradient_step(p, carry):
            probs = s_buf[p] * inverse
            dprobs = nt(pair_of(v_ref, p), gs[...])
            ds = (probs * (dprobs - delta)).astype(BF)
            dq_t[...] += nn(pair_of(k_ref, p).T, ds)
            dk = nn(ds, qs[...])
            dv = nn(probs.astype(BF), gs[...])
            for i, first in enumerate(starts(p)):
                here = pl.ds(first, BT)
                acc_k[here, :] += dk[i * BT : (i + 1) * BT]
                acc_v[here, :] += dv[i * BT : (i + 1) * BT]
            return carry

        lax.fori_loop(0, pairs, gradient_step, 0)
        for h in range(HEADS):
            dq_ref[rows, cols(h)] = (dq_t[:, cols(h)] * FACTOR).T.astype(BF)

    @pl.loop(0, total_blocks)
    def _(j):
        here = pl.ds(pl.multiple_of(j * BT, BT), BT)
        chip = j // 4
        at = (
            lax.rem(j // 2, 2), chip // SIDE, lax.rem(chip, SIDE),
            pl.ds(pl.multiple_of(lax.rem(j, 2) * BT, BT), BT),
        )
        tk_ref[at] = (acc_k[here, :] * FACTOR).astype(BF)
        tv_ref[at] = acc_v[here, :].astype(BF)


def attention(mask, q, g, keys, values):
    local, wide = q.shape
    total = keys.shape[0]
    width = HEADS * BT
    return pl.pallas_call(
        attention_kernel,
        out_shape=(
            jax.ShapeDtypeStruct((local, wide), F32),
            jax.ShapeDtypeStruct((local, wide), BF),
            jax.ShapeDtypeStruct((2, SIDE, SIDE, local, HW), BF),
            jax.ShapeDtypeStruct((2, SIDE, SIDE, local, HW), BF),
        ),
        in_specs=[SM, VM, VM, VM, VM],
        out_specs=(VM, VM, VM, VM),
        scratch_shapes=[
            pltpu.VMEM((MOST_PAIRS, 2 * BT, width), F32),
            pltpu.VMEM((total, HW), F32),
            pltpu.VMEM((total, HW), F32),
            pltpu.VMEM((width, HW), BF),
            pltpu.VMEM((width, HW), BF),
            pltpu.VMEM((HW, width), F32),
            pltpu.VMEM((HW, width), F32),
            pltpu.VMEM((HW, width), F32),
            pltpu.SMEM((total // BT + 8,), jnp.int32),
        ],
        compiler_params=pltpu.CompilerParams(vmem_limit_bytes=56 << 20),
        cost_estimate=pl.CostEstimate(
            flops=12 * 24 * 1024 * 128 * 128 * 2, bytes_accessed=12 << 20, transcendentals=1 << 22
        ),
        name="attention",
    )(mask, q, g, keys, values)


def ssm_local_kernel(
    x_ref, g_ref, b_ref, c_ref, step_ref, rate_ref, skip_ref,
    y_ref, dx_ref, xt_ref, eg_ref, send_ref, decay_ref, db_ref, dc_ref, cum_ref, rate_out, skip_out,
    dl, sum00, sum11, sum10,
):
    lanes = lax.broadcasted_iota(jnp.int32, (BT, BT), 1)
    subs = lax.broadcasted_iota(jnp.int32, (BT, BT), 0)
    lower = subs >= lanes
    tri = lower.astype(F32)
    dl[...] = jnp.zeros_like(dl)
    for h in range(HEADS):
        rate = jnp.exp(jnp.full((1, 1), rate_ref[h], F32))
        dl[:, h : h + 1] = -step_ref[:, h : h + 1] * rate
    run = []
    for i in range(2):
        run.append(
            lax.dot_general(
                tri, dl[i * BT : (i + 1) * BT, :], (((1,), (0,)), ((), ())),
                precision=HIGH, preferred_element_type=F32,
            )
        )
    run0, run1 = run
    end0, end1 = run0[BT - 1 : BT, :], run1[BT - 1 : BT, :]
    whole = end0 + end1
    run0_t, run1_t = run0.T, run1.T
    from_start = jnp.concatenate([run0, run1 + end0], axis=0)
    to_end = jnp.concatenate([end0 - run0 + end1, end1 - run1], axis=0)
    cum_ref[0] = from_start
    cum_ref[1] = to_end
    decay_ref[...] = jnp.broadcast_to(whole, decay_ref.shape)

    b0, b1 = b_ref[0:BT, :], b_ref[BT : 2 * BT, :]
    c0, c1 = c_ref[0:BT, :], c_ref[BT : 2 * BT, :]
    cb00, cb11, cb10 = nt(c0, b0), nt(c1, b1), nt(c1, b0)
    sum00[...] = jnp.zeros_like(sum00)
    sum11[...] = jnp.zeros_like(sum11)
    sum10[...] = jnp.zeros_like(sum10)
    b_t, c_t = b_ref[...].T, c_ref[...].T
    for h in range(HEADS):
        x0, x1 = x_ref[0:BT, cols(h)], x_ref[BT : 2 * BT, cols(h)]
        g0, g1 = g_ref[0:BT, cols(h)], g_ref[BT : 2 * BT, cols(h)]
        gain = skip_ref[h]
        col0, col1 = run0[:, h : h + 1], run1[:, h : h + 1]
        row0, row1 = run0_t[h : h + 1, :], run1_t[h : h + 1, :]
        last0 = end0[:, h : h + 1]

        def part(spread, cb, xs, gs, total, diagonal):
            if diagonal:
                decay = jnp.where(lower, jnp.exp(jnp.where(lower, spread, 0.0)), 0.0)
            else:
                decay = jnp.exp(spread)
            mixed = decay * cb
            outer = nt(gs, xs)
            total[...] += decay * outer
            terms = spread * (mixed * outer)
            mixed = mixed.astype(BF)
            return nn(mixed, xs), tn(mixed, gs), jnp.sum(terms, axis=0, keepdims=True)

        y00, dx00, r00 = part(col0 - row0, cb00, x0, g0, sum00, True)
        y11, dx11, r11 = part(col1 - row1, cb11, x1, g1, sum11, True)
        y10, dx10, r10 = part(col1 + (last0 - row0), cb10, x0, g1, sum10, False)
        rate_out[h : h + 1, :] = r00 + r11 + r10
        xf0, xf1, gf0, gf1 = x0.astype(F32), x1.astype(F32), g0.astype(F32), g1.astype(F32)
        skip_out[h : h + 1, :] = jnp.sum(xf0 * gf0 + xf1 * gf1, axis=0, keepdims=True)
        y_ref[0:BT, cols(h)] = y00 + gain * xf0
        y_ref[BT : 2 * BT, cols(h)] = y11 + y10 + gain * xf1
        dx_ref[0:BT, cols(h)] = dx00 + dx10 + gain * gf0
        dx_ref[BT : 2 * BT, cols(h)] = dx11 + gain * gf1
        start = jnp.exp(from_start[:, h : h + 1])
        tail = jnp.exp(to_end[:, h : h + 1])
        xt = (tail * jnp.concatenate([xf0, xf1], axis=0)).astype(BF)
        eg = (start * jnp.concatenate([gf0, gf1], axis=0)).astype(BF)
        xt_ref[:, cols(h)] = xt
        eg_ref[:, cols(h)] = eg
        end_state = nn(b_t, xt).astype(BF)
        start_grad = nn(c_t, eg).astype(BF)
        for quarter in range(4):
            at = slice(quarter * 32, quarter * 32 + 32)
            send_ref[h * 4 + quarter, 0] = end_state[at]
            send_ref[h * 4 + quarter, 1] = start_grad[at]
    s00, s11, s10 = sum00[...].astype(BF), sum11[...].astype(BF), sum10[...].astype(BF)
    dc_ref[0:BT, :] = nn(s00, b0)
    dc_ref[BT : 2 * BT, :] = nn(s11, b1) + nn(s10, b0)
    db_ref[0:BT, :] = tn(s00, c0) + tn(s10, c1)
    db_ref[BT : 2 * BT, :] = tn(s11, c1)


def ssm_local(x, g, b, c, step, rate_log, skip):
    local, wide = x.shape
    sds = jax.ShapeDtypeStruct
    return pl.pallas_call(
        ssm_local_kernel,
        out_shape=(
            sds((local, wide), F32),
            sds((local, wide), F32),
            sds((local, wide), BF),
            sds((local, wide), BF),
            sds((32, 2, 32, HW), BF),
            sds((8, HW), F32),
            sds((local, HW), F32),
            sds((local, HW), F32),
            sds((2, local, HW), F32),
            sds((HEADS, HW), F32),
            sds((HEADS, HW), F32),
        ),
        in_specs=[VM, VM, VM, VM, VM, SM, SM],
        out_specs=(VM,) * 11,
        scratch_shapes=[
            pltpu.VMEM((local, HW), F32),
            pltpu.VMEM((BT, BT), F32),
            pltpu.VMEM((BT, BT), F32),
            pltpu.VMEM((BT, BT), F32),
        ],
        compiler_params=pltpu.CompilerParams(vmem_limit_bytes=32 << 20),
        cost_estimate=pl.CostEstimate(flops=1 << 30, bytes_accessed=6 << 20, transcendentals=1 << 19),
        name="ssm_local",
    )(x, g, b, c, step, rate_log, skip)


def exchange_kernel(
    send_ref, decay_ref, out_ref,
    got, decays, back, s1, r1, s2, r2, s3, r3,
):
    n = 32
    me = lax.axis_index("seq")
    barrier = pltpu.get_barrier_semaphore()

    @pl.loop(1, n)
    def _(r):
        to = lax.rem(me + r, n)
        pl.semaphore_signal(barrier, inc=1, device_id={"seq": to}, device_id_type=MESH)

    pl.semaphore_wait(barrier, n - 1)

    def state_copy(r):
        to = lax.rem(me + r, n)
        return pltpu.make_async_remote_copy(
            src_ref=send_ref.at[to], dst_ref=got.at[me],
            send_sem=s1.at[r], recv_sem=r1.at[r],
            device_id={"seq": to}, device_id_type=MESH,
        )

    def decay_copy(r):
        to = lax.rem(me + r, n)
        return pltpu.make_async_remote_copy(
            src_ref=decay_ref, dst_ref=decays.at[me],
            send_sem=s2.at[r], recv_sem=r2.at[r],
            device_id={"seq": to}, device_id_type=MESH,
        )

    def back_copy(r):
        to = lax.rem(me + r, n)
        return pltpu.make_async_remote_copy(
            src_ref=back.at[to], dst_ref=out_ref.at[me],
            send_sem=s3.at[r], recv_sem=r3.at[r],
            device_id={"seq": to}, device_id_type=MESH,
        )

    @pl.loop(1, n)
    def _(r):
        decay_copy(r).start()
        state_copy(r).start()

    got[me] = send_ref[me]
    decays[me] = decay_ref[...]

    @pl.loop(1, n)
    def _(r):
        decay_copy(r).wait()
        state_copy(r).wait()

    head = me // 4
    lanes = lax.broadcasted_iota(jnp.int32, (8, HW), 1)

    def decay_of(d):
        only = jnp.where(lanes == head, decays[d], 0.0)
        return jnp.exp(jnp.sum(only, axis=1, keepdims=True))[0:1, :]

    def forward(d, state):
        back[d, 0] = state.astype(BF)
        return decay_of(d) * state + got[d, 0].astype(F32)

    def backward(k, state):
        d = n - 1 - k
        back[d, 1] = state.astype(BF)
        return decay_of(d) * state + got[d, 1].astype(F32)

    zero = jnp.zeros((32, HW), F32)
    lax.fori_loop(0, n, forward, zero)
    lax.fori_loop(0, n, backward, zero)

    @pl.loop(1, n)
    def _(r):
        back_copy(r).start()

    out_ref[me] = back[me]

    @pl.loop(1, n)
    def _(r):
        back_copy(r).wait()


def exchange(send, decay):
    n = 32
    dma = pltpu.SemaphoreType.DMA((n,))
    return pl.pallas_call(
        exchange_kernel,
        out_shape=jax.ShapeDtypeStruct((n, 2, 32, HW), BF),
        in_specs=[VM, VM],
        out_specs=VM,
        scratch_shapes=[
            pltpu.VMEM((n, 2, 32, HW), BF),
            pltpu.VMEM((n, 8, HW), F32),
            pltpu.VMEM((n, 2, 32, HW), BF),
            dma, dma, dma, dma, dma, dma,
        ],
        compiler_params=pltpu.CompilerParams(
            collective_id=1, has_side_effects=True, vmem_limit_bytes=16 << 20
        ),
        cost_estimate=pl.CostEstimate(flops=1 << 20, bytes_accessed=8 << 20, transcendentals=0),
        name="exchange",
    )(send, decay)


def ssm_finish_kernel(
    st_ref, y_ref, dx_ref, xt_ref, eg_ref, send_ref, decay_ref, db_ref, dc_ref, cum_ref,
    rate_in, b_ref, c_ref, x_ref, g_ref,
    yo_ref, dxo_ref, dbo_ref, dco_ref, rate_out,
):
    del send_ref
    dc = dc_ref[...]
    db = db_ref[...]
    for h in range(HEADS):
        s_in = jnp.concatenate([st_ref[h * 4 + i, 0] for i in range(4)], axis=0)
        g_out = jnp.concatenate([st_ref[h * 4 + i, 1] for i in range(4)], axis=0)
        log_start, log_tail = cum_ref[0][:, h : h + 1], cum_ref[1][:, h : h + 1]
        y_in = jnp.exp(log_start) * nn(c_ref[...], s_in)
        dx_in = jnp.exp(log_tail) * nn(b_ref[...], g_out)
        yo_ref[:, cols(h)] = y_ref[:, cols(h)] + y_in
        dxo_ref[:, cols(h)] = (dx_ref[:, cols(h)] + dx_in).astype(BF)
        dc = dc + nt(eg_ref[:, cols(h)], s_in)
        db = db + nt(xt_ref[:, cols(h)], g_out)
        gf, xf = g_ref[:, cols(h)].astype(F32), x_ref[:, cols(h)].astype(F32)
        terms = jnp.sum(log_start * (gf * y_in) + log_tail * (xf * dx_in), axis=0, keepdims=True)
        whole = decay_ref[0:1, h : h + 1]
        both = jnp.sum(s_in.astype(F32) * g_out.astype(F32), axis=0, keepdims=True)
        rate_out[h : h + 1, :] = rate_in[h : h + 1, :] + terms + whole * jnp.exp(whole) * both
    dco_ref[...] = dc.astype(BF)
    dbo_ref[...] = db.astype(BF)


def ssm_finish(states, y, dx, xt, eg, send, decay, db, dc, cum, rate, b, c, x, g):
    local, wide = x.shape
    sds = jax.ShapeDtypeStruct
    return pl.pallas_call(
        ssm_finish_kernel,
        out_shape=(
            sds((local, wide), F32),
            sds((local, wide), BF),
            sds((local, HW), BF),
            sds((local, HW), BF),
            sds((HEADS, HW), F32),
        ),
        in_specs=[VM] * 15,
        out_specs=(VM,) * 5,
        compiler_params=pltpu.CompilerParams(vmem_limit_bytes=32 << 20),
        cost_estimate=pl.CostEstimate(flops=1 << 28, bytes_accessed=6 << 20, transcendentals=1 << 10),
        name="ssm_finish",
    )(states, y, dx, xt, eg, send, decay, db, dc, cum, rate, b, c, x, g)


SIDE = 4
CHIPS = SIDE * SIDE


def place():
    me = lax.axis_index("seq")
    core = lax.rem(me, 2)
    chip = me // 2
    return me, chip // SIDE, lax.rem(chip, SIDE), core


def ring(a, step):
    return lax.rem(a + step + SIDE, SIDE)


def greet(me, x, y, core):
    barrier = pltpu.get_barrier_semaphore()
    friends = [
        (ring(x, 1), y, core), (ring(x, -1), y, core),
        (x, ring(y, 1), core), (x, ring(y, -1), core), (x, y, 1 - core),
    ]
    for a, b, c in friends:
        pl.semaphore_signal(
            barrier, inc=1, device_id={"seq": (a * SIDE + b) * 2 + c}, device_id_type=MESH
        )
    pl.semaphore_wait(barrier, len(friends))


class Copies:
    def __init__(self, send_sem, recv_sem):
        self.send_sem, self.recv_sem, self.made = send_sem, recv_sem, []

    def start(self, src, dst, device):
        at = len(self.made)
        copy = pltpu.make_async_remote_copy(
            src_ref=src, dst_ref=dst, send_sem=self.send_sem.at[at], recv_sem=self.recv_sem.at[at],
            device_id={"seq": device}, device_id_type=MESH,
        )
        copy.start()
        self.made.append(copy)
        return copy

    def finish(self):
        for copy in self.made:
            copy.wait_send()


LOW, UP = pl.ds(0, BT), pl.ds(BT, BT)
GATHER_COPIES = 2 * (22 + 16)


class GatherPart:
    def __init__(self, copies, own, out, first, second, at, core):
        self.c, self.own, self.out = copies, own, out
        self.f, self.s, self.at, self.core = first, second, at, core

    def dev(self, df, ds, other=False):
        core = 1 - self.core if other else self.core
        return self.at(ring(self.f, df), ring(self.s, ds)) * 2 + core

    def block(self, df, ds):
        return self.out.at[self.dev(df, ds)]

    def sibling(self, df, ds, src=None):
        here = self.block(df, ds)
        return self.c.start(here if src is None else src, here, self.dev(0, 0, True))

    def begin(self):
        mine = self.block(0, 0)
        self.a_up = self.c.start(self.own, mine, self.dev(1, 0))
        self.a_down = self.c.start(self.own, mine, self.dev(-1, 0))
        self.col = {0: self.column(0, self.own)}
        self.sib = [self.sibling(0, 0, self.own)]

    def column(self, df, src=None):
        here = self.block(df, 0)
        src = here if src is None else src
        return self.c.start(src, here, self.dev(0, 1)), self.c.start(src, here, self.dev(0, -1))

    def near(self):
        self.a_up.wait_recv()
        here = self.block(-1, 0)
        self.b_up = self.c.start(here.at[LOW], here.at[LOW], self.dev(1, 0))
        self.col[-1] = self.column(-1)
        self.sib.append(self.sibling(-1, 0))
        self.a_down.wait_recv()
        here = self.block(1, 0)
        self.b_down = self.c.start(here.at[UP], here.at[UP], self.dev(-1, 0))
        self.col[1] = self.column(1)
        self.sib.append(self.sibling(1, 0))
        self.last = []

    def pass_on(self, df):
        up, down = self.col[df]
        up.wait_recv()
        here = self.block(df, -1)
        one = self.c.start(here.at[LOW], here.at[LOW], self.dev(0, 1))
        self.sib.append(self.sibling(df, -1))
        down.wait_recv()
        here = self.block(df, 1)
        two = self.c.start(here.at[UP], here.at[UP], self.dev(0, -1))
        self.sib.append(self.sibling(df, 1))
        self.last.append((df, one, two))

    def far(self):
        self.b_up.wait_recv()
        self.b_down.wait_recv()
        self.col[2] = self.column(2)
        self.sib.append(self.sibling(2, 0))

    def end(self, i):
        df, one, two = self.last[i]
        one.wait_recv()
        two.wait_recv()
        self.sib.append(self.sibling(df, 2))


def gather_kernel(k_ref, v_ref, ko_ref, vo_ref, send_sem, recv_sem, own_sem):
    me, x, y, core = place()
    greet(me, x, y, core)
    copies = Copies(send_sem, recv_sem)
    parts = (
        GatherPart(copies, k_ref, ko_ref, x, y, lambda f, s: f * SIDE + s, core),
        GatherPart(copies, v_ref, vo_ref, y, x, lambda f, s: s * SIDE + f, core),
    )
    for part in parts:
        part.begin()
    own = [
        pltpu.make_async_copy(k_ref, ko_ref.at[me], own_sem.at[0]),
        pltpu.make_async_copy(v_ref, vo_ref.at[me], own_sem.at[1]),
    ]
    for copy in own:
        copy.start()
    for part in parts:
        part.near()
    for part in parts:
        part.pass_on(0)
    for part in parts:
        part.far()
    for df in (-1, 1, 2):
        for part in parts:
            part.pass_on(df)
    for i in range(4):
        for part in parts:
            part.end(i)
    for copy in own:
        copy.wait()
    for part in parts:
        for copy in part.sib:
            copy.wait_recv()
    copies.finish()


def gather(k, v):
    local = k.shape[0]
    full = jax.ShapeDtypeStruct((2 * CHIPS, local, HW), BF)
    dma = pltpu.SemaphoreType.DMA((GATHER_COPIES,))
    return pl.pallas_call(
        gather_kernel,
        out_shape=(full, full),
        in_specs=[VM, VM],
        out_specs=(VM, VM),
        scratch_shapes=[dma, dma, pltpu.SemaphoreType.DMA((2,))],
        compiler_params=pltpu.CompilerParams(
            collective_id=2, has_side_effects=True, vmem_limit_bytes=16 << 20
        ),
        cost_estimate=pl.CostEstimate(flops=1 << 20, bytes_accessed=8 << 20, transcendentals=0),
        name="gather",
    )(k, v)


SCATTER_COPIES = 2 * 16


class ScatterPart:
    def __init__(self, copies, terms, sib, acc, near, far, fin, near2, far2, out, first, second, x_first, core, dev):
        self.c, self.terms, self.sib, self.acc = copies, terms, sib, acc
        self.near, self.far, self.fin, self.near2, self.far2, self.out = near, far, fin, near2, far2, out
        self.f, self.s, self.x_first, self.core, self.dev = first, second, x_first, core, dev

    def chunk(self, ref, ds, core=None):
        s = ring(self.s, ds)
        ref = ref if core is None else ref.at[core]
        return ref.at[:, s] if self.x_first else ref.at[s]

    def begin(self):
        self.sibs = {}
        for ds in (2, 1, -1, 0):
            self.sibs[ds] = self.c.start(
                self.chunk(self.terms, ds, 1 - self.core), self.chunk(self.sib, ds), self.dev(0, 0, True)
            )

    def own(self, ds, rows):
        mine = self.chunk(self.terms, ds, self.core)[:, rows, :].astype(F32)
        return mine + self.chunk(self.sib, ds)[:, rows, :].astype(F32)

    def put(self, ds, rows, extra=None):
        value = self.own(ds, rows)
        if extra is not None:
            value = value + extra.astype(F32)
        self.chunk(self.acc, ds)[:, rows, :] = value.astype(BF)

    def one(self):
        self.sibs[2].wait_recv()
        for rows in (LOW, UP):
            self.put(2, rows)
        here = self.chunk(self.acc, 2)
        self.far_up = self.c.start(here.at[:, LOW], self.far.at[0], self.dev(0, 1))
        self.far_down = self.c.start(here.at[:, UP], self.far.at[1], self.dev(0, -1))

    def two(self):
        self.sibs[1].wait_recv()
        self.put(1, UP)
        self.up_a = self.c.start(
            self.chunk(self.acc, 1).at[:, UP], self.near.at[0, :, UP], self.dev(0, 1)
        )
        self.sibs[-1].wait_recv()
        self.put(-1, LOW)
        self.down_a = self.c.start(
            self.chunk(self.acc, -1).at[:, LOW], self.near.at[1, :, LOW], self.dev(0, -1)
        )

    def three(self):
        self.far_up.wait_recv()
        self.put(1, LOW, self.far[0])
        self.up_b = self.c.start(
            self.chunk(self.acc, 1).at[:, LOW], self.near.at[0, :, LOW], self.dev(0, 1)
        )
        self.far_down.wait_recv()
        self.put(-1, UP, self.far[1])
        self.down_b = self.c.start(
            self.chunk(self.acc, -1).at[:, UP], self.near.at[1, :, UP], self.dev(0, -1)
        )

    def four(self):
        self.sibs[0].wait_recv()
        for copy in (self.up_a, self.down_a, self.up_b, self.down_b):
            copy.wait_recv()
        for rows in (LOW, UP):
            total = self.own(0, rows) + self.near[0, :, rows, :].astype(F32) + self.near[1, :, rows, :].astype(F32)
            self.fin[:, rows, :] = total.astype(BF)
        here = self.fin.at[ring(self.f, 2)]
        self.far_up = self.c.start(here.at[LOW], self.far2.at[0], self.dev(1, 0))
        self.far_down = self.c.start(here.at[UP], self.far2.at[1], self.dev(-1, 0))
        self.up_a = self.c.start(
            self.fin.at[ring(self.f, 1)].at[UP], self.near2.at[0, UP], self.dev(1, 0)
        )
        self.down_a = self.c.start(
            self.fin.at[ring(self.f, -1)].at[LOW], self.near2.at[1, LOW], self.dev(-1, 0)
        )

    def five(self):
        self.far_up.wait_recv()
        here = self.fin.at[ring(self.f, 1)]
        here[LOW, :] = (here[LOW, :].astype(F32) + self.far2[0].astype(F32)).astype(BF)
        self.up_b = self.c.start(here.at[LOW], self.near2.at[0, LOW], self.dev(1, 0))
        self.far_down.wait_recv()
        here = self.fin.at[ring(self.f, -1)]
        here[UP, :] = (here[UP, :].astype(F32) + self.far2[1].astype(F32)).astype(BF)
        self.down_b = self.c.start(here.at[UP], self.near2.at[1, UP], self.dev(-1, 0))

    def six(self):
        for copy in (self.up_a, self.down_a, self.up_b, self.down_b):
            copy.wait_recv()
        mine = self.fin.at[self.f][...].astype(F32)
        self.out[...] = (mine + self.near2[0].astype(F32) + self.near2[1].astype(F32)).astype(BF)


def scatter_kernel(
    tk_ref, tv_ref, dk_ref, dv_ref,
    sib_k, sib_v, acc_k, acc_v, near_k, near_v, far_k, far_v, fin_k, fin_v,
    near2_k, near2_v, far2_k, far2_v, send_sem, recv_sem,
):
    me, x, y, core = place()
    greet(me, x, y, core)
    copies = Copies(send_sem, recv_sem)

    def dev_k(df, ds, other=False):
        c = 1 - core if other else core
        return (ring(x, df) * SIDE + ring(y, ds)) * 2 + c

    def dev_v(df, ds, other=False):
        c = 1 - core if other else core
        return (ring(x, ds) * SIDE + ring(y, df)) * 2 + c

    parts = (
        ScatterPart(copies, tk_ref, sib_k, acc_k, near_k, far_k, fin_k, near2_k, far2_k, dk_ref, x, y, True, core, dev_k),
        ScatterPart(copies, tv_ref, sib_v, acc_v, near_v, far_v, fin_v, near2_v, far2_v, dv_ref, y, x, False, core, dev_v),
    )
    for stage in ("begin", "one", "two", "three", "four", "five", "six"):
        for part in parts:
            getattr(part, stage)()
    copies.finish()


def scatter(tk, tv):
    local = tk.shape[3]
    out = jax.ShapeDtypeStruct((local, HW), BF)
    dma = pltpu.SemaphoreType.DMA((SCATTER_COPIES,))
    square = pltpu.VMEM((SIDE, SIDE, local, HW), BF)
    near = pltpu.VMEM((2, SIDE, local, HW), BF)
    far = pltpu.VMEM((2, SIDE, BT, HW), BF)
    fin = pltpu.VMEM((SIDE, local, HW), BF)
    near2 = pltpu.VMEM((2, local, HW), BF)
    far2 = pltpu.VMEM((2, BT, HW), BF)
    return pl.pallas_call(
        scatter_kernel,
        out_shape=(out, out),
        in_specs=[VM, VM],
        out_specs=(VM, VM),
        scratch_shapes=[
            square, square, square, square, near, near, far, far, fin, fin,
            near2, near2, far2, far2, dma, dma,
        ],
        compiler_params=pltpu.CompilerParams(
            collective_id=3, has_side_effects=True, vmem_limit_bytes=32 << 20
        ),
        cost_estimate=pl.CostEstimate(flops=1 << 20, bytes_accessed=8 << 20, transcendentals=0),
        name="scatter",
    )(tk, tv)


def body(query, key, value, ssm_input, in_b, in_c, step, rate_log, skip, block_mask, grad_out):
    q, k, v, x, b, c, g = (
        a[0] for a in (query, key, value, ssm_input, in_b, in_c, grad_out)
    )
    local = q.shape[0]
    keys, values = gather(k, v)
    keys, values = keys.reshape(-1, HW), values.reshape(-1, HW)
    y, dx, xt, eg, send, decay, db, dc, cum, rate, skip_terms = ssm_local(
        x, g, b, c, step[0], rate_log, skip
    )
    states = exchange(send, decay)
    y, dx, db, dc, rate = ssm_finish(
        states, y, dx, xt, eg, send, decay, db, dc, cum, rate, b, c, x, g
    )
    attended, dq, terms_k, terms_v = attention(block_mask[0], q, g, keys, values)
    dk, dv = scatter(terms_k, terms_v)
    rate_sum, skip_sum = lax.psum(
        (jnp.sum(rate, axis=1), jnp.sum(skip_terms, axis=1)), ("dp", "seq")
    )
    tokens = lax.axis_size("dp") * lax.axis_size("seq") * local
    layer_out = (attended + y).astype(BF)
    return (
        layer_out[None],
        dq[None],
        dk[None],
        dv[None],
        dx[None],
        db[None],
        dc[None],
        rate_sum / tokens,
        skip_sum / (tokens * HW),
    )


def solution(mesh):
    row = P("dp", "seq", None)
    in_specs = (row,) * 7 + (P(), P(), P("dp", None, None), row)
    out_specs = (row,) * 7 + (P(), P())
    return jax.shard_map(body, mesh=mesh, in_specs=in_specs, out_specs=out_specs, check_vma=False)
```

profile of v0, /device:TPU:1, one launch (start us, length us, event | category | flops | bytes accessed | tf_op | source)
XLA Modules:
  0.0 226.8 jit_solution(16008795329631713658)
XLA Ops:
  0.6 1.5 copy.20
  2.1 0.0 copy-start.4
  2.1 1.0 copy-done.4
  3.2 0.0 copy-start.6
  3.2 1.0 copy-done.6
  4.2 0.0 copy-start.14
  4.2 0.9 copy-done.14
  5.1 0.0 copy-start.15
  5.1 0.8 copy-done.15
  6.0 0.0 copy-start.17
  6.0 0.8 copy-done.17
  6.8 0.0 copy-start.23
  6.8 0.7 copy-done.23
  7.5 0.7 copy-done.24
  8.1 3.1 %ssm_local.1 = (f32[256,1024]{1,0:T(8,128)S(1)}, f32[256,1024]{1,0:T(8,128)S(1)}, bf16[256,1024]{1,0:T(8,128)(2,1)S(1)}, bf16[256,1024]{1,0:T(8,128)(2,1)S(1)}, ...) custom-call(bf16[256,1024]{1,0:T(8,128)(2,1)S(1)} %bitcast.19, ...), custom_call_target="tpu_custom_call" | custom-call | flops 1073741824 | bytes 6291456 | tf_op jit(solution)/shard_map/ssm_local/pallas_call | solution.py:257
  11.2 0.0 copy-start.2
  11.2 1.0 copy-done.2
  12.2 0.8 copy-done.8
  13.0 0.8 copy-done.10
  13.8 0.7 copy-done.12
  14.5 0.1 reduce_sum.19
  14.6 34.0 %exchange.1.st_ref = bf16[32,2,32,128]{3,2,1,0:T(8,128)(2,1)S(1)} custom-call(bf16[32,2,32,128]{3,2,1,0:T(8,128)(2,1)S(1)} %get-tuple-element.36.send_ref, f32[8,128]{1,0:T(8,128)S(1)} %get-tuple-element.37.decay_ref), custom_call_target="tpu_custom_call" | custom-call | flops 1048576 | bytes 8388608 | tf_op jit(solution)/shard_map/exchange/pallas_call | solution.py:372
  48.6 0.0 copy-done.5
  48.6 0.0 copy-start.3
  48.6 1.2 copy-done.3
  49.8 1.0 copy-done.7
  50.8 1.0 copy-done.9
  51.9 1.0 copy-done.11
  52.9 0.9 copy-done.13
  53.8 0.8 copy-done.16
  54.7 0.8 copy-done.18
  55.5 2.3 %ssm_finish.1 = (f32[256,1024]{1,0:T(8,128)S(1)}, bf16[256,1024]{1,0:T(8,128)(2,1)}, bf16[256,128]{1,0:T(8,128)(2,1)}, bf16[256,128]{1,0:T(8,128)(2,1)}, f32[8,128]{1,0:T(8,128)S(1)}) custom-call(bf16[32,2,32,128]{3,2,1,0:T(8,128)(2,1)S(1)} %exchange.1.st_ref, f32[256,1024]{1,0:T(8,128)S(1)} %get-tuple-element.38.y_ref, f32[256,1024]{1,0:T(8,128)S(1)} %copy-done.3, ...), custom_call_target="tpu_custom_call" | custom-call | flops 268435456 | bytes 6291456 | tf_op jit(solution)/shard_map/ssm_finish/pallas_call | solution.py:421
  57.8 0.1 reduce_sum.18
  57.9 78.1 %all-reduce = (f32[8]{0:T(128)S(1)}, f32[8]{0:T(128)S(1)}) all-reduce(f32[8]{0:T(128)S(1)} %reduce_sum.18, f32[8]{0:T(128)S(1)} %reduce_sum.19), channel_id=1, replica_groups=mesh['dp'=8,'seq'=32] {'dp','seq'}, use_global_device_ids=true, to_apply=%region_1.0 | all-reduce | flops 16 | bytes 128 | tf_op jit(solution)/shard_map/psum | solution.py:776
  136.0 0.5 broadcast_multiply_fusion
  136.6 0.8 copy-done.19
  137.4 0.8 copy-done.20
  138.2 21.3 %gather.1 = (bf16[32,256,128]{2,1,0:T(8,128)(2,1)S(1)}, bf16[32,256,128]{2,1,0:T(8,128)(2,1)S(1)}) custom-call(bf16[256,128]{1,0:T(8,128)(2,1)S(1)} %bitcast.29, bf16[256,128]{1,0:T(8,128)(2,1)S(1)} %bitcast.30), custom_call_target="tpu_custom_call" | custom-call | flops 1048576 | bytes 8388608 | tf_op jit(solution)/shard_map/gather/pallas_call | solution.py:595
  159.6 0.0 copy-start.21
  159.6 1.3 copy-done.21
  160.9 1.3 copy-done.22
  162.2 12.3 %attention.1 = (f32[256,1024]{1,0:T(8,128)}, bf16[256,1024]{1,0:T(8,128)(2,1)}, bf16[2,4,4,256,128]{4,3,2,1,0:T(8,128)(2,1)}, bf16[2,4,4,256,128]{4,3,2,1,0:T(8,128)(2,1)}) custom-call(s32[64,64]{1,0:T(8,128)} %bitcast.39, bf16[256,1024]{1,0:T(8,128)(2,1)} %bitcast.35, bf16[256,1024]{1,0:T(8,128)(2,1)} %bitcast.21, bf16[8192,128]{1,0:T(8,128)(2,1)} %bitcast.33, ...), custom_call_target="tpu_custom_call" | custom-call | flops 9663676416 | bytes 12582912 | tf_op jit(solution)/shard_map/attention/pallas_call | solution.py:138
  174.5 2.3 %fusion = bf16[1,256,1024]{2,1,0:T(8,128)(2,1)} fusion(f32[256,1024]{1,0:T(8,128)} %get-tuple-element.35, f32[256,1024]{1,0:T(8,128)S(1)} %get-tuple-element.46), kind=kLoop, calls=%fused_computation.1 | loop fusion | flops 524288 | bytes 2621440 | tf_op jit(solution)/shard_map/broadcast_in_dim | solution.py:782
  176.8 0.0 copy-done
  176.8 1.6 copy-done.1
  178.4 47.2 %scatter.1 = (bf16[256,128]{1,0:T(8,128)(2,1)S(1)}, bf16[256,128]{1,0:T(8,128)(2,1)S(1)}) custom-call(bf16[2,4,4,256,128]{4,3,2,1,0:T(8,128)(2,1)S(1)} %copy-done, bf16[2,4,4,256,128]{4,3,2,1,0:T(8,128)(2,1)S(1)} %copy-done.1), custom_call_target="tpu_custom_call" | custom-call | flops 1048576 | bytes 8388608 | tf_op jit(solution)/shard_map/scatter/pallas_call | solution.py:743
  225.5 0.6 copy.23
  226.2 0.6 copy.24
  (16 shorter events, 0.0 us)
Async XLA Ops:
  2.1 1.0 copy-start.4
  3.2 1.0 copy-start.6
  4.2 0.9 copy-start.14
  5.1 0.8 copy-start.15
  6.0 0.8 copy-start.17
  6.8 0.7 copy-start.23
  7.5 0.7 copy-start.24
  8.1 40.5 %copy-start.5 = (bf16[1,256,1024]{2,1,0:T(8,128)(2,1)S(1)}, bf16[1,256,1024]{2,1,0:T(8,128)(2,1)}, u32[]{:S(2)}) copy-start(bf16[1,256,1024]{2,1,0:T(8,128)(2,1)} %param.14) | copy-start | bytes 1572868
  11.2 1.0 copy-start.2
  12.2 0.8 copy-start.8
  13.0 0.8 copy-start.10
  13.8 0.7 copy-start.12
  48.6 1.2 copy-start.3
  49.8 1.0 copy-start.7
  50.8 1.0 copy-start.9
  51.9 1.0 copy-start.11
  52.9 0.9 copy-start.13
  53.8 0.8 copy-start.16
  54.7 0.8 copy-start.18
  136.5 0.8 copy-start.19
  137.4 0.8 copy-start.20
  159.6 1.3 copy-start.21
  160.9 1.3 copy-start.22
  174.5 2.3 %copy-start = (bf16[2,4,4,256,128]{4,3,2,1,0:T(8,128)(2,1)S(1)}, bf16[2,4,4,256,128]{4,3,2,1,0:T(8,128)(2,1)}, u32[]{:S(2)}) copy-start(bf16[2,4,4,256,128]{4,3,2,1,0:T(8,128)(2,1)} %get-tuple-element.48.tk_ref) | copy-start | bytes 6291460
  176.8 1.6 copy-start.1
where the time goes:
time: 229 us; the launch traced here: 227 us
  Pallas kernels  120 us (52%)
  blocking collectives  78.1 us (34%)
  local copies, waits for them, and re-layouts  24.8 us (11%)
  other arithmetic  3.04 us (1%)
    psum x1, blocking collectives, body(): lax.psum((jnp.sum(rate, axis=1), jnp.sum(skip_terms, axis=1)), ('dp', 'se...  78.1 us
    pallas_call x1, Pallas kernels, scatter(): pl.pallas_call(scatter_kernel, out_shape=(out, out), in_specs=[VM, VM], o...  47.2 us
    pallas_call x1, Pallas kernels, exchange(): pl.pallas_call(exchange_kernel, out_shape=jax.ShapeDtypeStruct((n, 2, 32,...  34 us
    unnamed x53, local copies, waits for them, and re-layouts  24.8 us
    pallas_call x1, Pallas kernels, gather(): pl.pallas_call(gather_kernel, out_shape=(full, full), in_specs=[VM, VM],...  21.3 us
    pallas_call x1, Pallas kernels, attention(): pl.pallas_call(attention_kernel, out_shape=(jax.ShapeDtypeStruct((local,...  12.3 us

commit v1 on v0

v1 whole, which is shorter than its diff:
```python
import functools

import jax
import jax.numpy as jnp
from jax import lax
from jax.experimental import pallas as pl
from jax.experimental.pallas import tpu as pltpu
from jax.sharding import PartitionSpec as P

HW = 128
HEADS = 8
BT = 128
MOST = 24
MOST_PAIRS = MOST // 2
FACTOR = HW ** (-0.5)
LOG2E = 1.4426950408889634
BF = jnp.bfloat16
F32 = jnp.float32
MESH = pl.DeviceIdType.MESH
HIGH = lax.Precision.HIGHEST

VM = pl.BlockSpec(memory_space=pltpu.VMEM)
HB = pl.BlockSpec(memory_space=pltpu.HBM)
SM = pl.BlockSpec(memory_space=pltpu.SMEM)


def nn(a, b):
    return lax.dot_general(a, b, (((1,), (0,)), ((), ())), preferred_element_type=F32)


def nt(a, b):
    return lax.dot_general(a, b, (((1,), (1,)), ((), ())), preferred_element_type=F32)


def tn(a, b):
    return lax.dot_general(a, b, (((0,), (0,)), ((), ())), preferred_element_type=F32)


def cols(h):
    return pl.ds(h * HW, HW)


def attention_kernel(
    mask_ref, q_ref, g_ref, k_ref, v_ref,
    o_ref, dq_ref, tk_ref, tv_ref,
    s_buf, acc_k, acc_v, qs, gs, g_t, o_t, dq_t, picked,
):
    total_blocks = mask_ref.shape[1]
    seq_at = lax.axis_index("seq")
    per_device = q_ref.shape[0] // BT
    acc_k[...] = jnp.zeros_like(acc_k)
    acc_v[...] = jnp.zeros_like(acc_v)

    @pl.loop(0, per_device)
    def _(block):
        row = seq_at * per_device + block

        def note(j, n):
            picked[n] = j
            return n + mask_ref[row, j]

        count = lax.fori_loop(0, total_blocks, note, jnp.int32(0))
        picked[count] = picked[0]
        pairs = (count + 1) // 2
        rows = pl.ds(pl.multiple_of(block * BT, BT), BT)
        for h in range(HEADS):
            qs[cols(h), :] = q_ref[rows, cols(h)]
            g_head = g_ref[rows, cols(h)]
            gs[cols(h), :] = g_head
            g_t[:, cols(h)] = g_head.astype(F32).T

        def starts(p):
            return tuple(pl.multiple_of(picked[2 * p + i] * BT, BT) for i in range(2))

        def pair_of(ref, p):
            first, second = starts(p)
            return jnp.concatenate([ref[pl.ds(first, BT), :], ref[pl.ds(second, BT), :]], axis=0)

        def score_step(p, top):
            s = nt(pair_of(k_ref, p), qs[...])
            bias = jnp.where(2 * p + 1 < count, 0.0, -1e30).astype(F32)
            s = jnp.concatenate([s[:BT], s[BT:] + bias], axis=0)
            s_buf[p] = s
            return jnp.maximum(top, jnp.max(s.reshape(-1, 8, s.shape[1]), axis=0))

        top = lax.fori_loop(
            0, pairs, score_step, jnp.full((8, HEADS * BT), -3e38, F32)
        )
        top = jnp.max(top, axis=0, keepdims=True)
        o_t[...] = jnp.zeros_like(o_t)

        def weight_step(p, total):
            w = jnp.exp2((s_buf[p] - top) * (FACTOR * LOG2E))
            s_buf[p] = w
            o_t[...] += nn(pair_of(v_ref, p).T, w.astype(BF))
            return total + jnp.sum(w.reshape(-1, 8, w.shape[1]), axis=0)

        total = lax.fori_loop(0, pairs, weight_step, jnp.zeros((8, HEADS * BT), F32))
        inverse = 1.0 / jnp.sum(total, axis=0, keepdims=True)
        o_t[...] = o_t[...] * inverse
        delta = jnp.sum(o_t[...] * g_t[...], axis=0, keepdims=True)
        for h in range(HEADS):
            o_ref[rows, cols(h)] = o_t[:, cols(h)].T
        dq_t[...] = jnp.zeros_like(dq_t)

        def gradient_step(p, carry):
            probs = s_buf[p] * inverse
            dprobs = nt(pair_of(v_ref, p), gs[...])
            ds = (probs * (dprobs - delta)).astype(BF)
            dq_t[...] += nn(pair_of(k_ref, p).T, ds)
            dk = nn(ds, qs[...])
            dv = nn(probs.astype(BF), gs[...])
            for i, first in enumerate(starts(p)):
                here = pl.ds(first, BT)
                acc_k[here, :] += dk[i * BT : (i + 1) * BT]
                acc_v[here, :] += dv[i * BT : (i + 1) * BT]
            return carry

        lax.fori_loop(0, pairs, gradient_step, 0)
        for h in range(HEADS):
            dq_ref[rows, cols(h)] = (dq_t[:, cols(h)] * FACTOR).T.astype(BF)

    @pl.loop(0, total_blocks)
    def _(j):
        here = pl.ds(pl.multiple_of(j * BT, BT), BT)
        chip = j // 4
        at = (
            lax.rem(j // 2, 2), chip // SIDE, lax.rem(chip, SIDE),
            pl.ds(pl.multiple_of(lax.rem(j, 2) * BT, BT), BT),
        )
        tk_ref[at] = (acc_k[here, :] * FACTOR).astype(BF)
        tv_ref[at] = acc_v[here, :].astype(BF)


def attention(mask, q, g, keys, values):
    local, wide = q.shape
    total = keys.shape[0]
    width = HEADS * BT
    return pl.pallas_call(
        attention_kernel,
        out_shape=(
            jax.ShapeDtypeStruct((local, wide), F32),
            jax.ShapeDtypeStruct((local, wide), BF),
            jax.ShapeDtypeStruct((2, SIDE, SIDE, local, HW), BF),
            jax.ShapeDtypeStruct((2, SIDE, SIDE, local, HW), BF),
        ),
        in_specs=[SM, VM, VM, VM, VM],
        out_specs=(VM, VM, VM, VM),
        scratch_shapes=[
            pltpu.VMEM((MOST_PAIRS, 2 * BT, width), F32),
            pltpu.VMEM((total, HW), F32),
            pltpu.VMEM((total, HW), F32),
            pltpu.VMEM((width, HW), BF),
            pltpu.VMEM((width, HW), BF),
            pltpu.VMEM((HW, width), F32),
            pltpu.VMEM((HW, width), F32),
            pltpu.VMEM((HW, width), F32),
            pltpu.SMEM((total // BT + 8,), jnp.int32),
        ],
        compiler_params=pltpu.CompilerParams(vmem_limit_bytes=36 << 20),
        cost_estimate=pl.CostEstimate(
            flops=12 * 24 * 1024 * 128 * 128 * 2, bytes_accessed=12 << 20, transcendentals=1 << 22
        ),
        name="attention",
    )(mask, q, g, keys, values)


SIDE = 4
CHIPS = SIDE * SIDE
PEERS = 2 * CHIPS
LAYERS = 8
QUARTER = 32
LOG_ROWS = 16
PACKED = 2 * QUARTER + LOG_ROWS


def place():
    me = lax.axis_index("seq")
    core = lax.rem(me, 2)
    chip = me // 2
    return me, chip // SIDE, lax.rem(chip, SIDE), core


def ring(a, step):
    return lax.rem(a + step + SIDE, SIDE)


def greet(me, also_dp):
    barrier = pltpu.get_barrier_semaphore()

    @pl.loop(1, PEERS)
    def _(r):
        to = lax.rem(me + r, PEERS)
        pl.semaphore_signal(barrier, inc=1, device_id={"seq": to}, device_id_type=MESH)

    waits = PEERS - 1
    if also_dp:
        layer = lax.axis_index("dp")

        @pl.loop(1, LAYERS)
        def _(r):
            to = lax.rem(layer + r, LAYERS)
            pl.semaphore_signal(barrier, inc=1, device_id={"dp": to}, device_id_type=MESH)

        waits += LAYERS - 1
    pl.semaphore_wait(barrier, waits)


def to_peers(me, src, dst, send_sem, recv_sem):
    def copy(r):
        to = lax.rem(me + r, PEERS)
        return pltpu.make_async_remote_copy(
            src_ref=src(to), dst_ref=dst, send_sem=send_sem.at[r], recv_sem=recv_sem.at[r],
            device_id={"seq": to}, device_id_type=MESH,
        )

    def start():
        @pl.loop(1, PEERS)
        def _(r):
            copy(r).start()

    def wait():
        @pl.loop(1, PEERS)
        def _(r):
            copy(r).wait()

    return start, wait


class Copies:
    def __init__(self, send_sem, recv_sem):
        self.send_sem, self.recv_sem, self.made = send_sem, recv_sem, []

    def start(self, src, dst, device):
        at = len(self.made)
        copy = pltpu.make_async_remote_copy(
            src_ref=src, dst_ref=dst, send_sem=self.send_sem.at[at], recv_sem=self.recv_sem.at[at],
            device_id={"seq": device}, device_id_type=MESH,
        )
        copy.start()
        self.made.append(copy)
        return copy

    def finish(self):
        for copy in self.made:
            copy.wait_send()


LOW, UP = pl.ds(0, BT), pl.ds(BT, BT)
GATHER_COPIES = 2 * (22 + 16)


class GatherPart:
    def __init__(self, copies, own, out, first, second, at, core):
        self.c, self.own, self.out = copies, own, out
        self.f, self.s, self.at, self.core = first, second, at, core

    def dev(self, df, ds, other=False):
        core = 1 - self.core if other else self.core
        return self.at(ring(self.f, df), ring(self.s, ds)) * 2 + core

    def block(self, df, ds):
        return self.out.at[self.dev(df, ds)]

    def sibling(self, df, ds, src=None):
        here = self.block(df, ds)
        return self.c.start(here if src is None else src, here, self.dev(0, 0, True))

    def begin(self):
        mine = self.block(0, 0)
        self.a_up = self.c.start(self.own, mine, self.dev(1, 0))
        self.a_down = self.c.start(self.own, mine, self.dev(-1, 0))
        self.col = {0: self.column(0, self.own)}
        self.sib = [self.sibling(0, 0, self.own)]

    def column(self, df, src=None):
        here = self.block(df, 0)
        src = here if src is None else src
        return self.c.start(src, here, self.dev(0, 1)), self.c.start(src, here, self.dev(0, -1))

    def near(self):
        self.a_up.wait_recv()
        here = self.block(-1, 0)
        self.b_up = self.c.start(here.at[LOW], here.at[LOW], self.dev(1, 0))
        self.col[-1] = self.column(-1)
        self.sib.append(self.sibling(-1, 0))
        self.a_down.wait_recv()
        here = self.block(1, 0)
        self.b_down = self.c.start(here.at[UP], here.at[UP], self.dev(-1, 0))
        self.col[1] = self.column(1)
        self.sib.append(self.sibling(1, 0))
        self.last = []

    def pass_on(self, df):
        up, down = self.col[df]
        up.wait_recv()
        here = self.block(df, -1)
        one = self.c.start(here.at[LOW], here.at[LOW], self.dev(0, 1))
        self.sib.append(self.sibling(df, -1))
        down.wait_recv()
        here = self.block(df, 1)
        two = self.c.start(here.at[UP], here.at[UP], self.dev(0, -1))
        self.sib.append(self.sibling(df, 1))
        self.last.append((df, one, two))

    def far(self):
        self.b_up.wait_recv()
        self.b_down.wait_recv()
        self.col[2] = self.column(2)
        self.sib.append(self.sibling(2, 0))

    def end(self, i):
        df, one, two = self.last[i]
        one.wait_recv()
        two.wait_recv()
        self.sib.append(self.sibling(df, 2))


def ssm_prepare(x_ref, step_ref, rate_ref, b_ref, c_ref, cum_ref, dl, bt_ref, ct_ref, sums):
    lanes = lax.broadcasted_iota(jnp.int32, (BT, BT), 1)
    subs = lax.broadcasted_iota(jnp.int32, (BT, BT), 0)
    upper = (subs <= lanes).astype(F32)
    dl[...] = jnp.zeros_like(dl)
    for h in range(HEADS):
        rate = jnp.exp(jnp.full((1, 1), rate_ref[h], F32))
        dl[h : h + 1, :] = -step_ref[h : h + 1, :] * rate
    run_t = []
    for i in range(2):
        run_t.append(
            lax.dot_general(
                dl[:, i * BT : (i + 1) * BT], upper, (((1,), (0,)), ((), ())),
                precision=HIGH, preferred_element_type=F32,
            )
        )
    run0, run1 = run_t[0].T, run_t[1].T
    end0, end1 = run0[BT - 1 : BT, :], run1[BT - 1 : BT, :]
    cum_ref[0] = jnp.concatenate([run0, run1 + end0], axis=0)
    cum_ref[1] = jnp.concatenate([end0 - run0 + end1, end1 - run1], axis=0)
    bt_ref[...] = b_ref[...].T
    ct_ref[...] = c_ref[...].T
    for total in sums:
        total[...] = jnp.zeros_like(total)
    b0, b1 = b_ref[0:BT, :], b_ref[BT : 2 * BT, :]
    c0, c1 = c_ref[0:BT, :], c_ref[BT : 2 * BT, :]
    return run0, run1, run_t[0], run_t[1], end0, end1, nt(c0, b0), nt(c1, b1), nt(c1, b0)


def split3(value):
    rows = lax.broadcasted_iota(jnp.int32, (LOG_ROWS, HW), 0)
    hi = value.astype(BF).astype(F32)
    mid = (value - hi).astype(BF).astype(F32)
    low = value - hi - mid
    out = jnp.where(rows == 0, hi, jnp.where(rows == 1, mid, jnp.where(rows == 2, low, 0.0)))
    return out.astype(BF)


def ssm_head(
    h, ready, x_ref, g_ref, skip_ref, cum_ref, bt_ref, ct_ref, sums,
    y_ref, dx_ref, xt_ref, eg_ref, send_ref, sums_ref,
):
    run0, run1, run0_t, run1_t, end0, end1, cb00, cb11, cb10 = ready
    sum00, sum11, sum10 = sums
    lanes = lax.broadcasted_iota(jnp.int32, (BT, BT), 1)
    subs = lax.broadcasted_iota(jnp.int32, (BT, BT), 0)
    lower = subs >= lanes
    x0, x1 = x_ref[0:BT, cols(h)], x_ref[BT : 2 * BT, cols(h)]
    g0, g1 = g_ref[0:BT, cols(h)], g_ref[BT : 2 * BT, cols(h)]
    gain = skip_ref[h]
    col0, col1 = run0[:, h : h + 1], run1[:, h : h + 1]
    row0, row1 = run0_t[h : h + 1, :], run1_t[h : h + 1, :]
    last0, last1 = end0[:, h : h + 1], end1[:, h : h + 1]

    def part(spread, cb, xs, gs, total, diagonal):
        if diagonal:
            decay = jnp.where(lower, jnp.exp(jnp.where(lower, spread, 0.0)), 0.0)
        else:
            decay = jnp.exp(spread)
        mixed = decay * cb
        outer = nt(gs, xs)
        total[...] += decay * outer
        terms = spread * (mixed * outer)
        mixed = mixed.astype(BF)
        return nn(mixed, xs), tn(mixed, gs), jnp.sum(terms, axis=0, keepdims=True)

    y00, dx00, r00 = part(col0 - row0, cb00, x0, g0, sum00, True)
    y11, dx11, r11 = part(col1 - row1, cb11, x1, g1, sum11, True)
    y10, dx10, r10 = part(col1 + (last0 - row0), cb10, x0, g1, sum10, False)
    xf0, xf1, gf0, gf1 = x0.astype(F32), x1.astype(F32), g0.astype(F32), g1.astype(F32)
    sums_ref[h : h + 1, :] = r00 + r11 + r10
    sums_ref[HEADS + h : HEADS + h + 1, :] = jnp.sum(xf0 * gf0 + xf1 * gf1, axis=0, keepdims=True)
    y_ref[0:BT, cols(h)] = y00 + gain * xf0
    y_ref[BT : 2 * BT, cols(h)] = y11 + y10 + gain * xf1
    dx_ref[0:BT, cols(h)] = dx00 + dx10 + gain * gf0
    dx_ref[BT : 2 * BT, cols(h)] = dx11 + gain * gf1
    start = jnp.exp(cum_ref[0][:, h : h + 1])
    tail = jnp.exp(cum_ref[1][:, h : h + 1])

    def state(turned, scaled, keep_ref):
        high = scaled.astype(BF)
        keep_ref[:, cols(h)] = high
        low = (scaled - high.astype(F32)).astype(BF)
        return (nn(turned, high) + nn(turned, low)).astype(BF)

    end_state = state(bt_ref[...], tail * jnp.concatenate([xf0, xf1], axis=0), xt_ref)
    start_grad = state(ct_ref[...], start * jnp.concatenate([gf0, gf1], axis=0), eg_ref)
    logs = split3(last0 + last1)
    for i in range(4):
        at = slice(i * QUARTER, (i + 1) * QUARTER)
        to = send_ref.at[h * 4 + i]
        to[0:QUARTER, :] = end_state[at]
        to[QUARTER : 2 * QUARTER, :] = start_grad[at]
        to[2 * QUARTER : PACKED, :] = logs


def ssm_end(b_ref, c_ref, sums, db_ref, dc_ref):
    s00, s11, s10 = (total[...].astype(BF) for total in sums)
    b0, b1 = b_ref[0:BT, :], b_ref[BT : 2 * BT, :]
    c0, c1 = c_ref[0:BT, :], c_ref[BT : 2 * BT, :]
    dc_ref[0:BT, :] = nn(s00, b0)
    dc_ref[BT : 2 * BT, :] = nn(s11, b1) + nn(s10, b0)
    db_ref[0:BT, :] = tn(s00, c0) + tn(s10, c1)
    db_ref[BT : 2 * BT, :] = tn(s11, c1)


def front_kernel(
    k_hbm, v_hbm, x_hbm, g_hbm, b_hbm, c_hbm, step_hbm, rate_hbm, skip_hbm,
    ko_ref, vo_ref, got_ref, y_ref, dx_ref, xt_ref, eg_ref, db_ref, dc_ref, cum_ref, sums_ref,
    x_ref, g_ref, b_ref, c_ref, step_ref, rate_ref, skip_ref, send_ref, dl, bt_ref, ct_ref, sum00, sum11, sum10,
    send_sem, recv_sem, own_sem, s1, r1,
):
    me, x, y, core = place()
    sources = (x_hbm, g_hbm, b_hbm, c_hbm, step_hbm, rate_hbm, skip_hbm)
    targets = (x_ref, g_ref, b_ref, c_ref, step_ref, rate_ref, skip_ref)
    loads = [
        pltpu.make_async_copy(src, dst, own_sem.at[i])
        for i, (src, dst) in enumerate(zip(sources, targets))
    ]
    for copy in loads:
        copy.start()
    greet(me, False)
    copies = Copies(send_sem, recv_sem)
    parts = (
        GatherPart(copies, k_hbm, ko_ref, x, y, lambda f, s: f * SIDE + s, core),
        GatherPart(copies, v_hbm, vo_ref, y, x, lambda f, s: s * SIDE + f, core),
    )
    for part in parts:
        part.begin()
    own = [
        pltpu.make_async_copy(k_hbm, ko_ref.at[me], own_sem.at[7]),
        pltpu.make_async_copy(v_hbm, vo_ref.at[me], own_sem.at[8]),
    ]
    for copy in own:
        copy.start()
    for copy in loads:
        copy.wait()

    def all_parts(name, *args):
        return lambda: [getattr(part, name)(*args) for part in parts]

    stages = {
        1: all_parts("near"), 3: all_parts("pass_on", 0), 5: all_parts("far"),
    }
    sums = (sum00, sum11, sum10)
    ready = ssm_prepare(x_ref, step_ref, rate_ref, b_ref, c_ref, cum_ref, dl, bt_ref, ct_ref, sums)
    for h in range(HEADS):
        ssm_head(
            h, ready, x_ref, g_ref, skip_ref, cum_ref, bt_ref, ct_ref, sums,
            y_ref, dx_ref, xt_ref, eg_ref, send_ref, sums_ref,
        )
        if h in stages:
            stages[h]()
    start, wait = to_peers(me, lambda to: send_ref.at[to], got_ref.at[me], s1, r1)
    start()
    got_ref[me] = send_ref[me]
    for df in (-1, 1, 2):
        for part in parts:
            part.pass_on(df)
    ssm_end(b_ref, c_ref, sums, db_ref, dc_ref)
    for i in range(4):
        for part in parts:
            part.end(i)
    for copy in own:
        copy.wait()
    for part in parts:
        for copy in part.sib:
            copy.wait_recv()
    copies.finish()
    wait()


def front(k, v, x, g, b, c, step_t, rate_log, skip):
    local, wide = x.shape
    sds = jax.ShapeDtypeStruct
    full = sds((PEERS, local, HW), BF)
    dma = pltpu.SemaphoreType.DMA
    return pl.pallas_call(
        front_kernel,
        out_shape=(
            full,
            full,
            sds((PEERS, PACKED, HW), BF),
            sds((local, wide), F32),
            sds((local, wide), F32),
            sds((local, wide), BF),
            sds((local, wide), BF),
            sds((local, HW), F32),
            sds((local, HW), F32),
            sds((2, local, HW), F32),
            sds((2 * HEADS, HW), F32),
        ),
        in_specs=[HB] * 9,
        out_specs=(VM,) * 11,
        scratch_shapes=[
            pltpu.VMEM((local, wide), BF),
            pltpu.VMEM((local, wide), BF),
            pltpu.VMEM((local, HW), BF),
            pltpu.VMEM((local, HW), BF),
            pltpu.VMEM((HEADS, local), F32),
            pltpu.SMEM((HEADS,), F32),
            pltpu.SMEM((HEADS,), F32),
            pltpu.VMEM((PEERS, PACKED, HW), BF),
            pltpu.VMEM((HW, local), F32),
            pltpu.VMEM((HW, local), BF),
            pltpu.VMEM((HW, local), BF),
            pltpu.VMEM((BT, BT), F32),
            pltpu.VMEM((BT, BT), F32),
            pltpu.VMEM((BT, BT), F32),
            dma((GATHER_COPIES,)),
            dma((GATHER_COPIES,)),
            dma((9,)),
            dma((PEERS,)),
            dma((PEERS,)),
        ],
        compiler_params=pltpu.CompilerParams(
            collective_id=1, has_side_effects=True, vmem_limit_bytes=14 << 20
        ),
        cost_estimate=pl.CostEstimate(flops=1 << 30, bytes_accessed=16 << 20, transcendentals=1 << 19),
        name="front",
    )(k, v, x, g, b, c, step_t, rate_log, skip)


SCATTER_COPIES = 2 * 16


class ScatterPart:
    def __init__(self, copies, terms, sib, acc, near, far, fin, near2, far2, out, first, second, x_first, core, dev):
        self.c, self.terms, self.sib, self.acc = copies, terms, sib, acc
        self.near, self.far, self.fin, self.near2, self.far2, self.out = near, far, fin, near2, far2, out
        self.f, self.s, self.x_first, self.core, self.dev = first, second, x_first, core, dev

    def chunk(self, ref, ds, core=None):
        s = ring(self.s, ds)
        ref = ref if core is None else ref.at[core]
        return ref.at[:, s] if self.x_first else ref.at[s]

    def begin(self):
        self.sibs = {}
        for ds in (2, 1, -1, 0):
            self.sibs[ds] = self.c.start(
                self.chunk(self.terms, ds, 1 - self.core), self.chunk(self.sib, ds), self.dev(0, 0, True)
            )

    def own(self, ds, rows):
        mine = self.chunk(self.terms, ds, self.core)[:, rows, :].astype(F32)
        return mine + self.chunk(self.sib, ds)[:, rows, :].astype(F32)

    def put(self, ds, rows, extra=None):
        value = self.own(ds, rows)
        if extra is not None:
            value = value + extra.astype(F32)
        self.chunk(self.acc, ds)[:, rows, :] = value.astype(BF)

    def one(self):
        self.sibs[2].wait_recv()
        for rows in (LOW, UP):
            self.put(2, rows)
        here = self.chunk(self.acc, 2)
        self.far_up = self.c.start(here.at[:, LOW], self.far.at[0], self.dev(0, 1))
        self.far_down = self.c.start(here.at[:, UP], self.far.at[1], self.dev(0, -1))

    def two(self):
        self.sibs[1].wait_recv()
        self.put(1, UP)
        self.up_a = self.c.start(
            self.chunk(self.acc, 1).at[:, UP], self.near.at[0, :, UP], self.dev(0, 1)
        )
        self.sibs[-1].wait_recv()
        self.put(-1, LOW)
        self.down_a = self.c.start(
            self.chunk(self.acc, -1).at[:, LOW], self.near.at[1, :, LOW], self.dev(0, -1)
        )

    def three(self):
        self.far_up.wait_recv()
        self.put(1, LOW, self.far[0])
        self.up_b = self.c.start(
            self.chunk(self.acc, 1).at[:, LOW], self.near.at[0, :, LOW], self.dev(0, 1)
        )
        self.far_down.wait_recv()
        self.put(-1, UP, self.far[1])
        self.down_b = self.c.start(
            self.chunk(self.acc, -1).at[:, UP], self.near.at[1, :, UP], self.dev(0, -1)
        )

    def four(self):
        self.sibs[0].wait_recv()
        for copy in (self.up_a, self.down_a, self.up_b, self.down_b):
            copy.wait_recv()
        for rows in (LOW, UP):
            total = self.own(0, rows) + self.near[0, :, rows, :].astype(F32) + self.near[1, :, rows, :].astype(F32)
            self.fin[:, rows, :] = total.astype(BF)
        here = self.fin.at[ring(self.f, 2)]
        self.far_up = self.c.start(here.at[LOW], self.far2.at[0], self.dev(1, 0))
        self.far_down = self.c.start(here.at[UP], self.far2.at[1], self.dev(-1, 0))
        self.up_a = self.c.start(
            self.fin.at[ring(self.f, 1)].at[UP], self.near2.at[0, UP], self.dev(1, 0)
        )
        self.down_a = self.c.start(
            self.fin.at[ring(self.f, -1)].at[LOW], self.near2.at[1, LOW], self.dev(-1, 0)
        )

    def five(self):
        self.far_up.wait_recv()
        here = self.fin.at[ring(self.f, 1)]
        here[LOW, :] = (here[LOW, :].astype(F32) + self.far2[0].astype(F32)).astype(BF)
        self.up_b = self.c.start(here.at[LOW], self.near2.at[0, LOW], self.dev(1, 0))
        self.far_down.wait_recv()
        here = self.fin.at[ring(self.f, -1)]
        here[UP, :] = (here[UP, :].astype(F32) + self.far2[1].astype(F32)).astype(BF)
        self.down_b = self.c.start(here.at[UP], self.near2.at[1, UP], self.dev(-1, 0))

    def six(self):
        for copy in (self.up_a, self.down_a, self.up_b, self.down_b):
            copy.wait_recv()
        mine = self.fin.at[self.f][...].astype(F32)
        self.out[...] = (mine + self.near2[0].astype(F32) + self.near2[1].astype(F32)).astype(BF)


def scan_states(me, got_ref, back_ref, kept, decays, logs, sums_ref):
    log_sum = jnp.sum(got_ref[:, 2 * QUARTER : PACKED, :].astype(F32), axis=1)
    logs[...] = log_sum
    decays[...] = jnp.exp(log_sum)

    def forward(d, state):
        kept[d] = state
        back_ref[d, 0] = state.astype(BF)
        return decays[pl.ds(d, 1), :] * state + got_ref[d, 0:QUARTER, :].astype(F32)

    def backward(k, carry):
        grad, rate = carry
        d = PEERS - 1 - k
        back_ref[d, 1] = grad.astype(BF)
        decay = decays[pl.ds(d, 1), :]
        rate = rate + (logs[pl.ds(d, 1), :] * decay) * (kept[d] * grad)
        return decay * grad + got_ref[d, QUARTER : 2 * QUARTER, :].astype(F32), rate

    zero = jnp.zeros((QUARTER, HW), F32)
    lax.fori_loop(0, PEERS, forward, zero)
    _, rate = lax.fori_loop(0, PEERS, backward, (zero, zero))
    rate = jnp.sum(rate, axis=0, keepdims=True)
    rows = lax.broadcasted_iota(jnp.int32, (2 * HEADS, HW), 0)
    sums_ref[...] += jnp.where(rows == me // 4, rate, 0.0)


def ssm_finish(
    st_ref, o_ref, y_ref, dx_ref, xt_ref, eg_ref, db_ref, dc_ref, cum_ref,
    b_ref, c_ref, x_ref, g_ref, out_ref, dxo_ref, dbo_ref, dco_ref, sums_ref,
):
    dc = dc_ref[...]
    db = db_ref[...]
    for h in range(HEADS):
        s_in = jnp.concatenate([st_ref[h * 4 + i, 0] for i in range(4)], axis=0)
        g_out = jnp.concatenate([st_ref[h * 4 + i, 1] for i in range(4)], axis=0)
        log_start, log_tail = cum_ref[0][:, h : h + 1], cum_ref[1][:, h : h + 1]
        y_in = jnp.exp(log_start) * nn(c_ref[...], s_in)
        dx_in = jnp.exp(log_tail) * nn(b_ref[...], g_out)
        out_ref[:, cols(h)] = (o_ref[:, cols(h)] + (y_ref[:, cols(h)] + y_in)).astype(BF)
        dxo_ref[:, cols(h)] = (dx_ref[:, cols(h)] + dx_in).astype(BF)
        dc = dc + nt(eg_ref[:, cols(h)], s_in)
        db = db + nt(xt_ref[:, cols(h)], g_out)
        gf, xf = g_ref[:, cols(h)].astype(F32), x_ref[:, cols(h)].astype(F32)
        terms = log_start * (gf * y_in) + log_tail * (xf * dx_in)
        sums_ref[h : h + 1, :] += jnp.sum(terms, axis=0, keepdims=True)
    dco_ref[...] = dc.astype(BF)
    dbo_ref[...] = db.astype(BF)


def back_kernel(
    tk_ref, tv_ref, got_ref, o_ref, y_ref, dx_ref, xt_ref, eg_ref, db_ref, dc_ref, cum_ref, sums_in,
    b_ref, c_ref, x_ref, g_ref,
    dk_ref, dv_ref, out_ref, dxo_ref, dbo_ref, dco_ref, total_ref,
    sib_k, sib_v, acc_k, acc_v, near_k, near_v, far_k, far_v, fin_k, fin_v,
    near2_k, near2_v, far2_k, far2_v,
    back_ref, st_ref, kept, decays, logs, sums_ref, seq_sums, seq_total, dp_sums,
    send_sem, recv_sem, s1, r1, s2, r2, s3, r3,
):
    me, x, y, core = place()
    layer = lax.axis_index("dp")
    greet(me, True)
    copies = Copies(send_sem, recv_sem)

    def dev_k(df, ds, other=False):
        c = 1 - core if other else core
        return (ring(x, df) * SIDE + ring(y, ds)) * 2 + c

    def dev_v(df, ds, other=False):
        c = 1 - core if other else core
        return (ring(x, ds) * SIDE + ring(y, df)) * 2 + c

    parts = (
        ScatterPart(copies, tk_ref, sib_k, acc_k, near_k, far_k, fin_k, near2_k, far2_k, dk_ref, x, y, True, core, dev_k),
        ScatterPart(copies, tv_ref, sib_v, acc_v, near_v, far_v, fin_v, near2_v, far2_v, dv_ref, y, x, False, core, dev_v),
    )

    def stage(name):
        for part in parts:
            getattr(part, name)()

    stage("begin")
    sums_ref[...] = sums_in[...]
    scan_states(me, got_ref, back_ref, kept, decays, logs, sums_ref)
    start, wait_states = to_peers(me, lambda to: back_ref.at[to], st_ref.at[me], s1, r1)
    stage("one")
    start()
    st_ref[me] = back_ref[me]
    stage("two")
    stage("three")
    wait_states()
    ssm_finish(
        st_ref, o_ref, y_ref, dx_ref, xt_ref, eg_ref, db_ref, dc_ref, cum_ref,
        b_ref, c_ref, x_ref, g_ref, out_ref, dxo_ref, dbo_ref, dco_ref, sums_ref,
    )
    start, wait_sums = to_peers(me, lambda to: sums_ref, seq_sums.at[me], s2, r2)
    start()
    seq_sums[me] = sums_ref[...]
    stage("four")
    stage("five")
    wait_sums()
    seq_total[...] = jnp.sum(seq_sums[...], axis=0)

    def dp_copy(r):
        to = lax.rem(layer + r, LAYERS)
        return pltpu.make_async_remote_copy(
            src_ref=seq_total, dst_ref=dp_sums.at[layer], send_sem=s3.at[r], recv_sem=r3.at[r],
            device_id={"dp": to}, device_id_type=MESH,
        )

    @pl.loop(1, LAYERS)
    def _(r):
        dp_copy(r).start()

    dp_sums[layer] = seq_total[...]
    stage("six")

    @pl.loop(1, LAYERS)
    def _(r):
        dp_copy(r).wait()

    total = jnp.sum(jnp.sum(dp_sums[...], axis=0), axis=1, keepdims=True)
    total_ref[...] = jnp.broadcast_to(total, total_ref.shape)
    copies.finish()


def back(tk, tv, got, o, y, dx, xt, eg, db, dc, cum, sums, b, c, x, g):
    local, wide = x.shape
    sds = jax.ShapeDtypeStruct
    small = sds((local, HW), BF)
    dma = pltpu.SemaphoreType.DMA
    square = pltpu.VMEM((SIDE, SIDE, local, HW), BF)
    near = pltpu.VMEM((2, SIDE, local, HW), BF)
    far = pltpu.VMEM((2, SIDE, BT, HW), BF)
    fin = pltpu.VMEM((SIDE, local, HW), BF)
    near2 = pltpu.VMEM((2, local, HW), BF)
    far2 = pltpu.VMEM((2, BT, HW), BF)
    states = pltpu.VMEM((PEERS, 2, QUARTER, HW), BF)
    tile = pltpu.VMEM((2 * HEADS, HW), F32)
    return pl.pallas_call(
        back_kernel,
        out_shape=(
            small, small, sds((local, wide), BF), sds((local, wide), BF), small, small,
            sds((2 * HEADS, HW), F32),
        ),
        in_specs=[VM] * 16,
        out_specs=(VM,) * 7,
        scratch_shapes=[
            square, square, square, square, near, near, far, far, fin, fin,
            near2, near2, far2, far2,
            states, states,
            pltpu.VMEM((PEERS, QUARTER, HW), F32),
            pltpu.VMEM((PEERS, HW), F32),
            pltpu.VMEM((PEERS, HW), F32),
            tile,
            pltpu.VMEM((PEERS, 2 * HEADS, HW), F32),
            tile,
            pltpu.VMEM((LAYERS, 2 * HEADS, HW), F32),
            dma((SCATTER_COPIES,)), dma((SCATTER_COPIES,)),
            dma((PEERS,)), dma((PEERS,)), dma((PEERS,)), dma((PEERS,)),
            dma((LAYERS,)), dma((LAYERS,)),
        ],
        compiler_params=pltpu.CompilerParams(
            collective_id=2, has_side_effects=True, vmem_limit_bytes=23 << 20
        ),
        cost_estimate=pl.CostEstimate(flops=1 << 29, bytes_accessed=16 << 20, transcendentals=1 << 12),
        name="back",
    )(tk, tv, got, o, y, dx, xt, eg, db, dc, cum, sums, b, c, x, g)


def emit_kernel(*refs):
    count = (len(refs) - 2) // 2
    total_ref, rate_ref = refs[count], refs[2 * count + 1]
    sem = refs[-1]
    moves = [
        pltpu.make_async_copy(refs[i], refs[count + 1 + i], sem.at[i]) for i in range(count)
    ]
    for move in moves:
        move.start()
    rate_ref[...] = total_ref[...]
    for move in moves:
        move.wait()


def emit(arrays, total):
    count = len(arrays)
    return pl.pallas_call(
        emit_kernel,
        out_shape=tuple(pltpu.HBM(a.shape, a.dtype) for a in arrays)
        + (jax.ShapeDtypeStruct(total.shape, total.dtype),),
        in_specs=[VM] * (count + 1),
        out_specs=(HB,) * count + (VM,),
        scratch_shapes=[pltpu.SemaphoreType.DMA((count,))],
        compiler_params=pltpu.CompilerParams(vmem_limit_bytes=4 << 20),
        cost_estimate=pl.CostEstimate(flops=0, bytes_accessed=3 << 20, transcendentals=0),
        name="emit",
    )(*arrays, total)


def body(query, key, value, ssm_input, in_b, in_c, step, rate_log, skip, block_mask, grad_out):
    q, k, v, x, b, c, g = (
        a[0] for a in (query, key, value, ssm_input, in_b, in_c, grad_out)
    )
    local = q.shape[0]
    fixed = [pltpu.with_memory_space_constraint(a, pltpu.HBM) for a in (k, v, x, g, b, c, step[0].T, rate_log, skip)]
    keys, values, got, *local_terms = front(*fixed)
    keys, values = keys.reshape(-1, HW), values.reshape(-1, HW)
    attended, dq, terms_k, terms_v = attention(block_mask[0], q, g, keys, values)
    dk, dv, layer_out, dx, db, dc, total = back(
        terms_k, terms_v, got, attended, *local_terms, b, c, x, g
    )
    layer_out, dx, dk, dv, db, dc, total = emit((layer_out, dx, dk, dv, db, dc), total)
    tokens = lax.axis_size("dp") * lax.axis_size("seq") * local
    return (
        layer_out[None],
        dq[None],
        dk[None],
        dv[None],
        dx[None],
        db[None],
        dc[None],
        total[:HEADS, 0] / tokens,
        total[HEADS:, 0] / (tokens * HW),
    )


def solution(mesh):
    row = P("dp", "seq", None)
    in_specs = (row,) * 7 + (P(), P(), P("dp", None, None), row)
    out_specs = (row,) * 7 + (P(), P())
    return jax.shard_map(body, mesh=mesh, in_specs=in_specs, out_specs=out_specs, check_vma=False)
```

time: 229 us -> 108 us (0.47); the launches traced: 227 us -> 108 us
  blocking collectives: 78.1 us -> 0 us
  local copies, waits for them, and re-layouts: 24.8 us -> 0.03 us
  Pallas kernels: 120 us -> 107 us
  other arithmetic: 3.04 us -> 0.66 us
    psum x1 -> x0, blocking collectives: 78.1 us -> none  [body(): lax.psum((jnp.sum(rate, axis=1), jnp.sum(skip_terms, axis=1)), ('dp', 'se...]
    unnamed x53 -> x12, local copies, waits for them, and re-layouts: 24.8 us -> 0.03 us
    pallas_call x5 -> x3, Pallas kernels: 108 us -> 97.9 us  [the longest x1 65 us: back(): pl.pallas_call(back_kernel, out_shape=(small, small, sds((local, wide), B...]
    pallas_call x1, Pallas kernels: 12.3 us -> 8.96 us  [attention(): pl.pallas_call(attention_kernel, out_shape=(jax.ShapeDtypeStruct((local,...]
    broadcast_in_dim x1 -> x0, other arithmetic: 2.29 us -> none  [body(): layer_out[None]]
where the time goes in v1:
time: 108 us
  Pallas kernels  107 us (99%)
    pallas_call x1, Pallas kernels, back(): pl.pallas_call(back_kernel, out_shape=(small, small, sds((local, wide), B...  65 us
    pallas_call x1, Pallas kernels, front(): pl.pallas_call(front_kernel, out_shape=(full, full, sds((PEERS, PACKED, H...  31.8 us
    pallas_call x1, Pallas kernels, attention(): pl.pallas_call(attention_kernel, out_shape=(jax.ShapeDtypeStruct((local,...  8.96 us

profile of v1, /device:TPU:1, one launch (start us, length us, event | category | flops | bytes accessed | tf_op | source)
XLA Modules:
  0.0 108.3 jit_solution(10073467572300096369)
XLA Ops:
  0.6 0.0 copy-start
  0.7 0.0 copy-start.5
  0.7 0.0 copy-start.4
  0.7 31.8 %front.1 = (bf16[32,256,128]{2,1,0:T(8,128)(2,1)S(1)}, bf16[32,256,128]{2,1,0:T(8,128)(2,1)S(1)}, bf16[32,80,128]{2,1,0:T(8,128)(2,1)S(1)}, f32[256,1024]{1,0:T(...) custom-call(bf16[256,128]{1,0:T(8,128)(2,1)} %bitcast.35, ...), custom_call_target="tpu_custom_call" | custom-call | flops 1073741824 | bytes 16777216 | tf_op jit(solution)/shard_map/front/pallas_call | solution.py:496
  32.4 0.0 copy-done
  32.5 0.0 copy-done.5
  32.5 0.0 copy-done.4
  32.5 0.0 copy-start.1
  32.5 0.0 copy-start.2
  32.5 0.0 copy-start.3
  32.5 9.0 %attention.1 = (f32[256,1024]{1,0:T(8,128)S(1)}, bf16[256,1024]{1,0:T(8,128)(2,1)}, bf16[2,4,4,256,128]{4,3,2,1,0:T(8,128)(2,1)S(1)}, bf16[2,4,4,256,128]{4,3,2,1,0:T(8,128)(2,1)S(1)}) custom-call(s32[64,64]{1,0:T(8,128)S(1)} %bitcast.30, bf16[256,1024]{1,0:T(8,128)(2,1)S(1)} %bitcast.29, bf16[256,1024]{1,0:T(8,128)(2,1)S(1)} %bitcast.21, ...), custom_call_target="tpu_custom_call" | custom-call | flops 9663676416 | bytes 12582912 | tf_op jit(solution)/shard_map/attention/pallas_call | solution.py:139
  41.5 0.0 copy-done.1
  41.5 0.0 copy-done.2
  41.5 0.0 copy-done.3
  41.5 65.0 %back.1 = (bf16[256,128]{1,0:T(8,128)(2,1)S(1)}, bf16[256,128]{1,0:T(8,128)(2,1)S(1)}, bf16[256,1024]{1,0:T(8,128)(2,1)S(1)}, bf16[256,1024]{1,0:T(8,128)(2,1)S(...) custom-call(bf16[2,4,4,256,128]{4,3,2,1,0:T(8,128)(2,1)S(1)} %get-tuple-element.40.tk_ref, ...), custom_call_target="tpu_custom_call" | custom-call | flops 536870912 | bytes 16777216 | tf_op jit(solution)/shard_map/back/pallas_call | solution.py:777
  106.5 1.1 %emit.1 = (bf16[256,1024]{1,0:T(8,128)(2,1)}, bf16[256,1024]{1,0:T(8,128)(2,1)}, bf16[256,128]{1,0:T(8,128)(2,1)}, bf16[256,128]{1,0:T(8,128)(2,1)}, bf16[256,12...) custom-call(bf16[256,1024]{1,0:T(8,128)(2,1)S(1)} %get-tuple-element.52.refs_0_, ...), custom_call_target="tpu_custom_call" | custom-call | bytes 3145728 | tf_op jit(solution)/shard_map/emit/pallas_call | solution.py:824
  107.6 0.7 multiply_reduce_fusion
Async XLA Ops:
  0.6 31.8 %copy-start = (bf16[1,256,1024]{2,1,0:T(8,128)(2,1)S(1)}, bf16[1,256,1024]{2,1,0:T(8,128)(2,1)}, u32[]{:S(2)}) copy-start(bf16[1,256,1024]{2,1,0:T(8,128)(2,1)} %param.21) | copy-start | bytes 1572868
  0.7 31.8 %copy-start.5 = (s32[1,64,64]{2,1,0:T(8,128)S(1)}, s32[1,64,64]{2,1,0:T(8,128)}, u32[]{:S(2)}) copy-start(s32[1,64,64]{2,1,0:T(8,128)} %param.20) | copy-start | bytes 49156
  0.7 31.8 %copy-start.4 = (bf16[1,256,1024]{2,1,0:T(8,128)(2,1)S(1)}, bf16[1,256,1024]{2,1,0:T(8,128)(2,1)}, u32[]{:S(2)}) copy-start(bf16[1,256,1024]{2,1,0:T(8,128)(2,1)} %param.11) | copy-start | bytes 1572868
  32.5 9.0 %copy-start.1 = (bf16[1,256,1024]{2,1,0:T(8,128)(2,1)S(1)}, bf16[1,256,1024]{2,1,0:T(8,128)(2,1)}, u32[]{:S(2)}) copy-start(bf16[1,256,1024]{2,1,0:T(8,128)(2,1)} %param.14) | copy-start | bytes 1572868
  32.5 9.0 %copy-start.2 = (bf16[1,256,128]{2,1,0:T(8,128)(2,1)S(1)}, bf16[1,256,128]{2,1,0:T(8,128)(2,1)}, u32[]{:S(2)}) copy-start(bf16[1,256,128]{2,1,0:T(8,128)(2,1)} %param.15) | copy-start | bytes 196612
  32.5 9.0 %copy-start.3 = (bf16[1,256,128]{2,1,0:T(8,128)(2,1)S(1)}, bf16[1,256,128]{2,1,0:T(8,128)(2,1)}, u32[]{:S(2)}) copy-start(bf16[1,256,128]{2,1,0:T(8,128)(2,1)} %param.16) | copy-start | bytes 196612

commit v2 on v1

--- a/solution.py
+++ b/solution.py
@@ -11,7 +11,8 @@
 HEADS = 8
 BT = 128
 MOST = 24
-MOST_PAIRS = MOST // 2
+WIDE = 8
+NARROW = 4
 FACTOR = HW ** (-0.5)
 LOG2E = 1.4426950408889634
 BF = jnp.bfloat16
@@ -59,9 +60,12 @@
             picked[n] = j
             return n + mask_ref[row, j]
 
-        count = lax.fori_loop(0, total_blocks, note, jnp.int32(0))
-        picked[count] = picked[0]
-        pairs = (count + 1) // 2
+        count = lax.fori_loop(0, total_blocks, note, jnp.int32(0), unroll=8)
+        for i in range(WIDE - 1):
+            picked[count + i] = picked[0]
+        rest = lax.rem(count, WIDE)
+        wide = count // WIDE + (rest > NARROW).astype(jnp.int32)
+        narrow = jnp.logical_and(rest > 0, rest <= NARROW).astype(jnp.int32)
         rows = pl.ds(pl.multiple_of(block * BT, BT), BT)
         for h in range(HEADS):
             qs[cols(h), :] = q_ref[rows, cols(h)]
@@ -69,33 +73,40 @@
             gs[cols(h), :] = g_head
             g_t[:, cols(h)] = g_head.astype(F32).T
 
-        def starts(p):
-            return tuple(pl.multiple_of(picked[2 * p + i] * BT, BT) for i in range(2))
-
-        def pair_of(ref, p):
-            first, second = starts(p)
-            return jnp.concatenate([ref[pl.ds(first, BT), :], ref[pl.ds(second, BT), :]], axis=0)
-
-        def score_step(p, top):
-            s = nt(pair_of(k_ref, p), qs[...])
-            bias = jnp.where(2 * p + 1 < count, 0.0, -1e30).astype(F32)
-            s = jnp.concatenate([s[:BT], s[BT:] + bias], axis=0)
-            s_buf[p] = s
+        def starts(at, size):
+            return tuple(pl.multiple_of(picked[at + i] * BT, BT) for i in range(size))
+
+        def group_of(ref, at, size):
+            return jnp.concatenate([ref[pl.ds(first, BT), :] for first in starts(at, size)], axis=0)
+
+        def over_groups(step, carry):
+            carry = lax.fori_loop(0, wide, lambda p, c: step(p * WIDE, WIDE, c), carry)
+            return lax.fori_loop(0, narrow, lambda p, c: step(wide * WIDE, NARROW, c), carry)
+
+        def flat(value):
+            return value.reshape(-1, value.shape[-1])
+
+        def score_step(at, size, top):
+            s = nt(group_of(k_ref, at, size), qs[...])
+            parts = [s[:BT]]
+            for i in range(1, size):
+                bias = jnp.where(at + i < count, 0.0, -1e30).astype(F32)
+                parts.append(s[i * BT : (i + 1) * BT] + bias)
+            s = jnp.concatenate(parts, axis=0)
+            s_buf[pl.ds(at, size)] = s.reshape(size, BT, -1)
             return jnp.maximum(top, jnp.max(s.reshape(-1, 8, s.shape[1]), axis=0))
 
-        top = lax.fori_loop(
-            0, pairs, score_step, jnp.full((8, HEADS * BT), -3e38, F32)
-        )
+        top = over_groups(score_step, jnp.full((8, HEADS * BT), -3e38, F32))
         top = jnp.max(top, axis=0, keepdims=True)
         o_t[...] = jnp.zeros_like(o_t)
 
-        def weight_step(p, total):
-            w = jnp.exp2((s_buf[p] - top) * (FACTOR * LOG2E))
-            s_buf[p] = w
-            o_t[...] += nn(pair_of(v_ref, p).T, w.astype(BF))
+        def weight_step(at, size, total):
+            w = jnp.exp2((flat(s_buf[pl.ds(at, size)]) - top) * (FACTOR * LOG2E))
+            s_buf[pl.ds(at, size)] = w.reshape(size, BT, -1)
+            o_t[...] += tn(group_of(v_ref, at, size), w.astype(BF))
             return total + jnp.sum(w.reshape(-1, 8, w.shape[1]), axis=0)
 
-        total = lax.fori_loop(0, pairs, weight_step, jnp.zeros((8, HEADS * BT), F32))
+        total = over_groups(weight_step, jnp.zeros((8, HEADS * BT), F32))
         inverse = 1.0 / jnp.sum(total, axis=0, keepdims=True)
         o_t[...] = o_t[...] * inverse
         delta = jnp.sum(o_t[...] * g_t[...], axis=0, keepdims=True)
@@ -103,20 +114,20 @@
             o_ref[rows, cols(h)] = o_t[:, cols(h)].T
         dq_t[...] = jnp.zeros_like(dq_t)
 
-        def gradient_step(p, carry):
-            probs = s_buf[p] * inverse
-            dprobs = nt(pair_of(v_ref, p), gs[...])
+        def gradient_step(at, size, carry):
+            probs = flat(s_buf[pl.ds(at, size)]) * inverse
+            dprobs = nt(group_of(v_ref, at, size), gs[...])
             ds = (probs * (dprobs - delta)).astype(BF)
-            dq_t[...] += nn(pair_of(k_ref, p).T, ds)
+            dq_t[...] += tn(group_of(k_ref, at, size), ds)
             dk = nn(ds, qs[...])
             dv = nn(probs.astype(BF), gs[...])
-            for i, first in enumerate(starts(p)):
+            for i, first in enumerate(starts(at, size)):
                 here = pl.ds(first, BT)
                 acc_k[here, :] += dk[i * BT : (i + 1) * BT]
                 acc_v[here, :] += dv[i * BT : (i + 1) * BT]
             return carry
 
-        lax.fori_loop(0, pairs, gradient_step, 0)
+        over_groups(gradient_step, 0)
         for h in range(HEADS):
             dq_ref[rows, cols(h)] = (dq_t[:, cols(h)] * FACTOR).T.astype(BF)
 
@@ -147,7 +158,7 @@
         in_specs=[SM, VM, VM, VM, VM],
         out_specs=(VM, VM, VM, VM),
         scratch_shapes=[
-            pltpu.VMEM((MOST_PAIRS, 2 * BT, width), F32),
+            pltpu.VMEM((MOST, BT, width), F32),
             pltpu.VMEM((total, HW), F32),
             pltpu.VMEM((total, HW), F32),
             pltpu.VMEM((width, HW), BF),
@@ -157,7 +168,7 @@
             pltpu.VMEM((HW, width), F32),
             pltpu.SMEM((total // BT + 8,), jnp.int32),
         ],
-        compiler_params=pltpu.CompilerParams(vmem_limit_bytes=36 << 20),
+        compiler_params=pltpu.CompilerParams(vmem_limit_bytes=38 << 20),
         cost_estimate=pl.CostEstimate(
             flops=12 * 24 * 1024 * 128 * 128 * 2, bytes_accessed=12 << 20, transcendentals=1 << 22
         ),
@@ -734,7 +745,6 @@
     start()
     seq_sums[me] = sums_ref[...]
     stage("four")
-    stage("five")
     wait_sums()
     seq_total[...] = jnp.sum(seq_sums[...], axis=0)
 
@@ -750,6 +760,7 @@
         dp_copy(r).start()
 
     dp_sums[layer] = seq_total[...]
+    stage("five")
     stage("six")
 
     @pl.loop(1, LAYERS)

time: 108 us -> 98.4 us (0.911)
  Pallas kernels: 107 us -> 96.9 us
    pallas_call x1, Pallas kernels: 65 us -> 54.1 us  [back(): pl.pallas_call(back_kernel, out_shape=(small, small, sds((local, wide), B...]
where the time goes in v2:
time: 98.4 us
  Pallas kernels  96.9 us (98%)
    pallas_call x1, Pallas kernels, back(): pl.pallas_call(back_kernel, out_shape=(small, small, sds((local, wide), B...  54.1 us
    pallas_call x1, Pallas kernels, front(): pl.pallas_call(front_kernel, out_shape=(full, full, sds((PEERS, PACKED, H...  31.8 us
    pallas_call x1, Pallas kernels, attention(): pl.pallas_call(attention_kernel, out_shape=(jax.ShapeDtypeStruct((local,...  9.96 us

profile of v2, /device:TPU:1, one launch (start us, length us, event | category | flops | bytes accessed | tf_op | source)
XLA Modules:
  0.0 98.4 jit_solution(15737517869386669064)
XLA Ops:
  0.6 0.0 copy-start
  0.7 0.0 copy-start.5
  0.7 0.0 copy-start.4
  0.7 31.8 %front.1 = (bf16[32,256,128]{2,1,0:T(8,128)(2,1)S(1)}, bf16[32,256,128]{2,1,0:T(8,128)(2,1)S(1)}, bf16[32,80,128]{2,1,0:T(8,128)(2,1)S(1)}, f32[256,1024]{1,0:T(...) custom-call(bf16[256,128]{1,0:T(8,128)(2,1)} %bitcast.35, ...), custom_call_target="tpu_custom_call" | custom-call | flops 1073741824 | bytes 16777216 | tf_op jit(solution)/shard_map/front/pallas_call | solution.py:507
  32.4 0.0 copy-done
  32.5 0.0 copy-done.5
  32.5 0.0 copy-done.4
  32.5 0.0 copy-start.1
  32.5 0.0 copy-start.2
  32.5 0.0 copy-start.3
  32.5 10.0 %attention.1 = (f32[256,1024]{1,0:T(8,128)S(1)}, bf16[256,1024]{1,0:T(8,128)(2,1)}, bf16[2,4,4,256,128]{4,3,2,1,0:T(8,128)(2,1)S(1)}, bf16[2,4,4,256,128]{4,3,2,1,0:T(8,128)(2,1)S(1)}) custom-call(s32[64,64]{1,0:T(8,128)S(1)} %bitcast.30, bf16[256,1024]{1,0:T(8,128)(2,1)S(1)} %bitcast.29, bf16[256,1024]{1,0:T(8,128)(2,1)S(1)} %bitcast.21, ...), custom_call_target="tpu_custom_call" | custom-call | flops 9663676416 | bytes 12582912 | tf_op jit(solution)/shard_map/attention/pallas_call | solution.py:150
  42.5 0.0 copy-done.1
  42.5 0.0 copy-done.2
  42.5 0.0 copy-done.3
  42.5 54.1 %back.1 = (bf16[256,128]{1,0:T(8,128)(2,1)S(1)}, bf16[256,128]{1,0:T(8,128)(2,1)S(1)}, bf16[256,1024]{1,0:T(8,128)(2,1)S(1)}, bf16[256,1024]{1,0:T(8,128)(2,1)S(...) custom-call(bf16[2,4,4,256,128]{4,3,2,1,0:T(8,128)(2,1)S(1)} %get-tuple-element.40.tk_ref, ...), custom_call_target="tpu_custom_call" | custom-call | flops 536870912 | bytes 16777216 | tf_op jit(solution)/shard_map/back/pallas_call | solution.py:788
  96.6 1.1 %emit.1 = (bf16[256,1024]{1,0:T(8,128)(2,1)}, bf16[256,1024]{1,0:T(8,128)(2,1)}, bf16[256,128]{1,0:T(8,128)(2,1)}, bf16[256,128]{1,0:T(8,128)(2,1)}, bf16[256,12...) custom-call(bf16[256,1024]{1,0:T(8,128)(2,1)S(1)} %get-tuple-element.52.refs_0_, ...), custom_call_target="tpu_custom_call" | custom-call | bytes 3145728 | tf_op jit(solution)/shard_map/emit/pallas_call | solution.py:835
  97.7 0.7 multiply_reduce_fusion
Async XLA Ops:
  0.6 31.8 %copy-start = (bf16[1,256,1024]{2,1,0:T(8,128)(2,1)S(1)}, bf16[1,256,1024]{2,1,0:T(8,128)(2,1)}, u32[]{:S(2)}) copy-start(bf16[1,256,1024]{2,1,0:T(8,128)(2,1)} %param.21) | copy-start | bytes 1572868
  0.7 31.8 %copy-start.5 = (s32[1,64,64]{2,1,0:T(8,128)S(1)}, s32[1,64,64]{2,1,0:T(8,128)}, u32[]{:S(2)}) copy-start(s32[1,64,64]{2,1,0:T(8,128)} %param.20) | copy-start | bytes 49156
  0.7 31.8 %copy-start.4 = (bf16[1,256,1024]{2,1,0:T(8,128)(2,1)S(1)}, bf16[1,256,1024]{2,1,0:T(8,128)(2,1)}, u32[]{:S(2)}) copy-start(bf16[1,256,1024]{2,1,0:T(8,128)(2,1)} %param.11) | copy-start | bytes 1572868
  32.5 10.0 %copy-start.1 = (bf16[1,256,1024]{2,1,0:T(8,128)(2,1)S(1)}, bf16[1,256,1024]{2,1,0:T(8,128)(2,1)}, u32[]{:S(2)}) copy-start(bf16[1,256,1024]{2,1,0:T(8,128)(2,1)} %param.14) | copy-start | bytes 1572868
  32.5 10.0 %copy-start.2 = (bf16[1,256,128]{2,1,0:T(8,128)(2,1)S(1)}, bf16[1,256,128]{2,1,0:T(8,128)(2,1)}, u32[]{:S(2)}) copy-start(bf16[1,256,128]{2,1,0:T(8,128)(2,1)} %param.15) | copy-start | bytes 196612
  32.5 10.0 %copy-start.3 = (bf16[1,256,128]{2,1,0:T(8,128)(2,1)S(1)}, bf16[1,256,128]{2,1,0:T(8,128)(2,1)}, u32[]{:S(2)}) copy-start(bf16[1,256,128]{2,1,0:T(8,128)(2,1)} %param.16) | copy-start | bytes 196612

commit v3 on v2

--- a/solution.py
+++ b/solution.py
@@ -196,15 +196,18 @@
     return lax.rem(a + step + SIDE, SIDE)
 
 
-def greet(me, also_dp):
+def greet(chip, core, also_dp):
     barrier = pltpu.get_barrier_semaphore()
 
-    @pl.loop(1, PEERS)
+    @pl.loop(1, CHIPS)
     def _(r):
-        to = lax.rem(me + r, PEERS)
+        to = lax.rem(chip + r, CHIPS) * 2 + core
         pl.semaphore_signal(barrier, inc=1, device_id={"seq": to}, device_id_type=MESH)
 
-    waits = PEERS - 1
+    pl.semaphore_signal(
+        barrier, inc=1, device_id={"seq": chip * 2 + 1 - core}, device_id_type=MESH
+    )
+    waits = CHIPS
     if also_dp:
         layer = lax.axis_index("dp")
 
@@ -217,25 +220,32 @@
     pl.semaphore_wait(barrier, waits)
 
 
-def to_peers(me, src, dst, send_sem, recv_sem):
+def to_peers(chip, core, src, dst, send_sem, recv_sem):
     def copy(r):
-        to = lax.rem(me + r, PEERS)
+        to = lax.rem(chip + r, CHIPS)
         return pltpu.make_async_remote_copy(
             src_ref=src(to), dst_ref=dst, send_sem=send_sem.at[r], recv_sem=recv_sem.at[r],
-            device_id={"seq": to}, device_id_type=MESH,
+            device_id={"seq": to * 2 + core}, device_id_type=MESH,
         )
 
     def start():
-        @pl.loop(1, PEERS)
+        @pl.loop(1, CHIPS)
         def _(r):
             copy(r).start()
 
     def wait():
-        @pl.loop(1, PEERS)
+        @pl.loop(1, CHIPS)
         def _(r):
             copy(r).wait()
 
     return start, wait
+
+
+def to_sibling(chip, core, src, dst, sems):
+    return pltpu.make_async_remote_copy(
+        src_ref=src, dst_ref=dst, send_sem=sems.at[0], recv_sem=sems.at[1],
+        device_id={"seq": chip * 2 + 1 - core}, device_id_type=MESH,
+    )
 
 
 class Copies:
@@ -417,7 +427,7 @@
     logs = split3(last0 + last1)
     for i in range(4):
         at = slice(i * QUARTER, (i + 1) * QUARTER)
-        to = send_ref.at[h * 4 + i]
+        to = send_ref.at[(h * 4 + i) % 2, (h * 4 + i) // 2]
         to[0:QUARTER, :] = end_state[at]
         to[QUARTER : 2 * QUARTER, :] = start_grad[at]
         to[2 * QUARTER : PACKED, :] = logs
@@ -433,11 +443,33 @@
     db_ref[BT : 2 * BT, :] = tn(s11, c1)
 
 
+def combine(core, send_ref, sib_ref, comb_ref):
+    first = (core == 0).astype(F32)
+    second = 1.0 - first
+    for h in range(HEADS):
+        at = pl.ds(2 * h, 2)
+        mine, other = send_ref[core, at].astype(F32), sib_ref[core, at].astype(F32)
+        log_mine = jnp.sum(mine[0, 2 * QUARTER :], axis=0, keepdims=True)
+        log_other = jnp.sum(other[0, 2 * QUARTER :], axis=0, keepdims=True)
+        by_mine, by_other = jnp.exp(log_mine), jnp.exp(log_other)
+        ends = slice(0, QUARTER)
+        comb_ref[at, ends, :] = (
+            (first * by_other + second) * mine[:, ends] + (first + second * by_mine) * other[:, ends]
+        ).astype(BF)
+        grads = slice(QUARTER, 2 * QUARTER)
+        comb_ref[at, grads, :] = (
+            (first + second * by_other) * mine[:, grads] + (first * by_mine + second) * other[:, grads]
+        ).astype(BF)
+        logs = split3(log_mine + log_other)
+        for i in range(2):
+            comb_ref[2 * h + i, 2 * QUARTER : PACKED, :] = logs
+
+
 def front_kernel(
     k_hbm, v_hbm, x_hbm, g_hbm, b_hbm, c_hbm, step_hbm, rate_hbm, skip_hbm,
-    ko_ref, vo_ref, got_ref, y_ref, dx_ref, xt_ref, eg_ref, db_ref, dc_ref, cum_ref, sums_ref,
-    x_ref, g_ref, b_ref, c_ref, step_ref, rate_ref, skip_ref, send_ref, dl, bt_ref, ct_ref, sum00, sum11, sum10,
-    send_sem, recv_sem, own_sem, s1, r1,
+    ko_ref, vo_ref, got_ref, sib_ref, y_ref, dx_ref, xt_ref, eg_ref, db_ref, dc_ref, cum_ref, sums_ref,
+    x_ref, g_ref, b_ref, c_ref, step_ref, rate_ref, skip_ref, send_ref, comb_ref, dl, bt_ref, ct_ref, sum00, sum11, sum10,
+    send_sem, recv_sem, own_sem, s1, r1, pair_sem,
 ):
     me, x, y, core = place()
     sources = (x_hbm, g_hbm, b_hbm, c_hbm, step_hbm, rate_hbm, skip_hbm)
@@ -448,7 +480,8 @@
     ]
     for copy in loads:
         copy.start()
-    greet(me, False)
+    chip = me // 2
+    greet(chip, core, False)
     copies = Copies(send_sem, recv_sem)
     parts = (
         GatherPart(copies, k_hbm, ko_ref, x, y, lambda f, s: f * SIDE + s, core),
@@ -480,13 +513,19 @@
         )
         if h in stages:
             stages[h]()
-    start, wait = to_peers(me, lambda to: send_ref.at[to], got_ref.at[me], s1, r1)
+    pair = to_sibling(chip, core, send_ref, sib_ref, pair_sem)
+    pair.start()
+    for part in parts:
+        part.pass_on(-1)
+    ssm_end(b_ref, c_ref, sums, db_ref, dc_ref)
+    pair.wait()
+    combine(core, send_ref, sib_ref, comb_ref)
+    start, wait = to_peers(chip, core, lambda to: comb_ref.at[to], got_ref.at[chip], s1, r1)
     start()
-    got_ref[me] = send_ref[me]
-    for df in (-1, 1, 2):
+    got_ref[chip] = comb_ref[chip]
+    for df in (1, 2):
         for part in parts:
             part.pass_on(df)
-    ssm_end(b_ref, c_ref, sums, db_ref, dc_ref)
     for i in range(4):
         for part in parts:
             part.end(i)
@@ -509,7 +548,8 @@
         out_shape=(
             full,
             full,
-            sds((PEERS, PACKED, HW), BF),
+            sds((CHIPS, PACKED, HW), BF),
+            sds((2, CHIPS, PACKED, HW), BF),
             sds((local, wide), F32),
             sds((local, wide), F32),
             sds((local, wide), BF),
@@ -520,7 +560,7 @@
             sds((2 * HEADS, HW), F32),
         ),
         in_specs=[HB] * 9,
-        out_specs=(VM,) * 11,
+        out_specs=(VM,) * 12,
         scratch_shapes=[
             pltpu.VMEM((local, wide), BF),
             pltpu.VMEM((local, wide), BF),
@@ -529,7 +569,8 @@
             pltpu.VMEM((HEADS, local), F32),
             pltpu.SMEM((HEADS,), F32),
             pltpu.SMEM((HEADS,), F32),
-            pltpu.VMEM((PEERS, PACKED, HW), BF),
+            pltpu.VMEM((2, CHIPS, PACKED, HW), BF),
+            pltpu.VMEM((CHIPS, PACKED, HW), BF),
             pltpu.VMEM((HW, local), F32),
             pltpu.VMEM((HW, local), BF),
             pltpu.VMEM((HW, local), BF),
@@ -539,8 +580,9 @@
             dma((GATHER_COPIES,)),
             dma((GATHER_COPIES,)),
             dma((9,)),
-            dma((PEERS,)),
-            dma((PEERS,)),
+            dma((CHIPS,)),
+            dma((CHIPS,)),
+            dma((2,)),
         ],
         compiler_params=pltpu.CompilerParams(
             collective_id=1, has_side_effects=True, vmem_limit_bytes=14 << 20
@@ -659,29 +701,45 @@
 
     def backward(k, carry):
         grad, rate = carry
-        d = PEERS - 1 - k
+        d = CHIPS - 1 - k
         back_ref[d, 1] = grad.astype(BF)
         decay = decays[pl.ds(d, 1), :]
         rate = rate + (logs[pl.ds(d, 1), :] * decay) * (kept[d] * grad)
         return decay * grad + got_ref[d, QUARTER : 2 * QUARTER, :].astype(F32), rate
 
     zero = jnp.zeros((QUARTER, HW), F32)
-    lax.fori_loop(0, PEERS, forward, zero)
-    _, rate = lax.fori_loop(0, PEERS, backward, (zero, zero))
+    lax.fori_loop(0, CHIPS, forward, zero)
+    _, rate = lax.fori_loop(0, CHIPS, backward, (zero, zero))
     rate = jnp.sum(rate, axis=0, keepdims=True)
     rows = lax.broadcasted_iota(jnp.int32, (2 * HEADS, HW), 0)
     sums_ref[...] += jnp.where(rows == me // 4, rate, 0.0)
 
 
 def ssm_finish(
-    st_ref, o_ref, y_ref, dx_ref, xt_ref, eg_ref, db_ref, dc_ref, cum_ref,
+    core, st_ref, sib_ref, o_ref, y_ref, dx_ref, xt_ref, eg_ref, db_ref, dc_ref, cum_ref,
     b_ref, c_ref, x_ref, g_ref, out_ref, dxo_ref, dbo_ref, dco_ref, sums_ref,
 ):
     dc = dc_ref[...]
     db = db_ref[...]
+    first = (core == 0).astype(F32)
+    second = 1.0 - first
     for h in range(HEADS):
-        s_in = jnp.concatenate([st_ref[h * 4 + i, 0] for i in range(4)], axis=0)
-        g_out = jnp.concatenate([st_ref[h * 4 + i, 1] for i in range(4)], axis=0)
+        owners = [((h * 4 + i) % 2, (h * 4 + i) // 2) for i in range(4)]
+
+        def joined(pick):
+            return jnp.concatenate([pick(*at) for at in owners], axis=0).astype(F32)
+
+        chip_state = joined(lambda a, b: st_ref[a, b, 0])
+        chip_grad = joined(lambda a, b: st_ref[a, b, 1])
+        sib_state = joined(lambda a, b: sib_ref[a, b, 0:QUARTER, :])
+        sib_grad = joined(lambda a, b: sib_ref[a, b, QUARTER : 2 * QUARTER, :])
+        sib_logs = sib_ref[0, 2 * h, 2 * QUARTER : PACKED, :].astype(F32)
+        sib_decay = jnp.exp(jnp.sum(sib_logs, axis=0, keepdims=True))
+        s_in = (first * chip_state + second * (sib_decay * chip_state + sib_state)).astype(BF)
+        g_out = (first * (sib_decay * chip_grad + sib_grad) + second * chip_grad).astype(BF)
+        across = jnp.sum(
+            first * (sib_grad * chip_state) + second * (chip_grad * sib_state), axis=0, keepdims=True
+        )
         log_start, log_tail = cum_ref[0][:, h : h + 1], cum_ref[1][:, h : h + 1]
         y_in = jnp.exp(log_start) * nn(c_ref[...], s_in)
         dx_in = jnp.exp(log_tail) * nn(b_ref[...], g_out)
@@ -691,23 +749,27 @@
         db = db + nt(xt_ref[:, cols(h)], g_out)
         gf, xf = g_ref[:, cols(h)].astype(F32), x_ref[:, cols(h)].astype(F32)
         terms = log_start * (gf * y_in) + log_tail * (xf * dx_in)
-        sums_ref[h : h + 1, :] += jnp.sum(terms, axis=0, keepdims=True)
+        whole = log_start[-1:, :]
+        sums_ref[h : h + 1, :] += (
+            jnp.sum(terms, axis=0, keepdims=True) + (whole * jnp.exp(whole)) * across
+        )
     dco_ref[...] = dc.astype(BF)
     dbo_ref[...] = db.astype(BF)
 
 
 def back_kernel(
-    tk_ref, tv_ref, got_ref, o_ref, y_ref, dx_ref, xt_ref, eg_ref, db_ref, dc_ref, cum_ref, sums_in,
+    tk_ref, tv_ref, got_ref, sib_ref, o_ref, y_ref, dx_ref, xt_ref, eg_ref, db_ref, dc_ref, cum_ref, sums_in,
     b_ref, c_ref, x_ref, g_ref,
     dk_ref, dv_ref, out_ref, dxo_ref, dbo_ref, dco_ref, total_ref,
     sib_k, sib_v, acc_k, acc_v, near_k, near_v, far_k, far_v, fin_k, fin_v,
     near2_k, near2_v, far2_k, far2_v,
-    back_ref, st_ref, kept, decays, logs, sums_ref, seq_sums, seq_total, dp_sums,
-    send_sem, recv_sem, s1, r1, s2, r2, s3, r3,
+    back_ref, st_ref, kept, decays, logs, sums_ref, sib_sums, chip_sums, seq_sums, seq_total, dp_sums,
+    send_sem, recv_sem, s1, r1, s2, r2, s3, r3, pair_sem, pair_sem2,
 ):
     me, x, y, core = place()
     layer = lax.axis_index("dp")
-    greet(me, True)
+    chip = me // 2
+    greet(chip, core, True)
     copies = Copies(send_sem, recv_sem)
 
     def dev_k(df, ds, other=False):
@@ -730,21 +792,31 @@
     stage("begin")
     sums_ref[...] = sums_in[...]
     scan_states(me, got_ref, back_ref, kept, decays, logs, sums_ref)
-    start, wait_states = to_peers(me, lambda to: back_ref.at[to], st_ref.at[me], s1, r1)
+    start, wait_states = to_peers(
+        chip, core, lambda to: back_ref.at[to], st_ref.at[core, chip], s1, r1
+    )
     stage("one")
     start()
-    st_ref[me] = back_ref[me]
+    st_ref[core, chip] = back_ref[chip]
     stage("two")
+    wait_states()
+    pair = to_sibling(chip, core, st_ref.at[core], st_ref.at[core], pair_sem)
+    pair.start()
     stage("three")
-    wait_states()
+    pair.wait()
     ssm_finish(
-        st_ref, o_ref, y_ref, dx_ref, xt_ref, eg_ref, db_ref, dc_ref, cum_ref,
+        core, st_ref, sib_ref, o_ref, y_ref, dx_ref, xt_ref, eg_ref, db_ref, dc_ref, cum_ref,
         b_ref, c_ref, x_ref, g_ref, out_ref, dxo_ref, dbo_ref, dco_ref, sums_ref,
     )
-    start, wait_sums = to_peers(me, lambda to: sums_ref, seq_sums.at[me], s2, r2)
+    pair = to_sibling(chip, core, sums_ref, sib_sums, pair_sem2)
+    pair.start()
+    stage("four")
+    pair.wait()
+    chip_sums[...] = sums_ref[...] + sib_sums[...]
+    start, wait_sums = to_peers(chip, core, lambda to: chip_sums, seq_sums.at[chip], s2, r2)
     start()
-    seq_sums[me] = sums_ref[...]
-    stage("four")
+    seq_sums[chip] = chip_sums[...]
+    stage("five")
     wait_sums()
     seq_total[...] = jnp.sum(seq_sums[...], axis=0)
 
@@ -760,7 +832,6 @@
         dp_copy(r).start()
 
     dp_sums[layer] = seq_total[...]
-    stage("five")
     stage("six")
 
     @pl.loop(1, LAYERS)
@@ -772,7 +843,7 @@
     copies.finish()
 
 
-def back(tk, tv, got, o, y, dx, xt, eg, db, dc, cum, sums, b, c, x, g):
+def back(tk, tv, got, sib, o, y, dx, xt, eg, db, dc, cum, sums, b, c, x, g):
     local, wide = x.shape
     sds = jax.ShapeDtypeStruct
     small = sds((local, HW), BF)
@@ -783,7 +854,6 @@
     fin = pltpu.VMEM((SIDE, local, HW), BF)
     near2 = pltpu.VMEM((2, local, HW), BF)
     far2 = pltpu.VMEM((2, BT, HW), BF)
-    states = pltpu.VMEM((PEERS, 2, QUARTER, HW), BF)
     tile = pltpu.VMEM((2 * HEADS, HW), F32)
     return pl.pallas_call(
         back_kernel,
@@ -791,29 +861,30 @@
             small, small, sds((local, wide), BF), sds((local, wide), BF), small, small,
             sds((2 * HEADS, HW), F32),
         ),
-        in_specs=[VM] * 16,
+        in_specs=[VM] * 17,
         out_specs=(VM,) * 7,
         scratch_shapes=[
             square, square, square, square, near, near, far, far, fin, fin,
             near2, near2, far2, far2,
-            states, states,
-            pltpu.VMEM((PEERS, QUARTER, HW), F32),
-            pltpu.VMEM((PEERS, HW), F32),
-            pltpu.VMEM((PEERS, HW), F32),
-            tile,
-            pltpu.VMEM((PEERS, 2 * HEADS, HW), F32),
+            pltpu.VMEM((CHIPS, 2, QUARTER, HW), BF),
+            pltpu.VMEM((2, CHIPS, 2, QUARTER, HW), BF),
+            pltpu.VMEM((CHIPS, QUARTER, HW), F32),
+            pltpu.VMEM((CHIPS, HW), F32),
+            pltpu.VMEM((CHIPS, HW), F32),
+            tile, tile, tile,
+            pltpu.VMEM((CHIPS, 2 * HEADS, HW), F32),
             tile,
             pltpu.VMEM((LAYERS, 2 * HEADS, HW), F32),
             dma((SCATTER_COPIES,)), dma((SCATTER_COPIES,)),
-            dma((PEERS,)), dma((PEERS,)), dma((PEERS,)), dma((PEERS,)),
-            dma((LAYERS,)), dma((LAYERS,)),
+            dma((CHIPS,)), dma((CHIPS,)), dma((CHIPS,)), dma((CHIPS,)),
+            dma((LAYERS,)), dma((LAYERS,)), dma((2,)), dma((2,)),
         ],
         compiler_params=pltpu.CompilerParams(
             collective_id=2, has_side_effects=True, vmem_limit_bytes=23 << 20
         ),
         cost_estimate=pl.CostEstimate(flops=1 << 29, bytes_accessed=16 << 20, transcendentals=1 << 12),
         name="back",
-    )(tk, tv, got, o, y, dx, xt, eg, db, dc, cum, sums, b, c, x, g)
+    )(tk, tv, got, sib, o, y, dx, xt, eg, db, dc, cum, sums, b, c, x, g)
 
 
 def emit_kernel(*refs):
@@ -851,11 +922,11 @@
     )
     local = q.shape[0]
     fixed = [pltpu.with_memory_space_constraint(a, pltpu.HBM) for a in (k, v, x, g, b, c, step[0].T, rate_log, skip)]
-    keys, values, got, *local_terms = front(*fixed)
+    keys, values, got, sib, *local_terms = front(*fixed)
     keys, values = keys.reshape(-1, HW), values.reshape(-1, HW)
     attended, dq, terms_k, terms_v = attention(block_mask[0], q, g, keys, values)
     dk, dv, layer_out, dx, db, dc, total = back(
-        terms_k, terms_v, got, attended, *local_terms, b, c, x, g
+        terms_k, terms_v, got, sib, attended, *local_terms, b, c, x, g
     )
     layer_out, dx, dk, dv, db, dc, total = emit((layer_out, dx, dk, dv, db, dc), total)
     tokens = lax.axis_size("dp") * lax.axis_size("seq") * local

time: 98.4 us -> 94 us (0.955); the launches traced: 98.4 us -> 92.6 us
  Pallas kernels: 96.9 us -> 91.1 us
    pallas_call x1, Pallas kernels: 54.1 us -> 49.7 us  [back(): pl.pallas_call(back_kernel, out_shape=(small, small, sds((local, wide), B...]
    pallas_call x1, Pallas kernels: 31.8 us -> 30.4 us  [front(): pl.pallas_call(front_kernel, out_shape=(full, full, sds((CHIPS, PACKED, H...]
where the time goes in v3:
time: 94 us; the launch traced here: 92.6 us
  Pallas kernels  91.1 us (97%)
    pallas_call x1, Pallas kernels, back(): pl.pallas_call(back_kernel, out_shape=(small, small, sds((local, wide), B...  49.7 us
    pallas_call x1, Pallas kernels, front(): pl.pallas_call(front_kernel, out_shape=(full, full, sds((CHIPS, PACKED, H...  30.4 us
    pallas_call x1, Pallas kernels, attention(): pl.pallas_call(attention_kernel, out_shape=(jax.ShapeDtypeStruct((local,...  9.95 us

profile of v3, /device:TPU:1, one launch (start us, length us, event | category | flops | bytes accessed | tf_op | source)
XLA Modules:
  0.0 92.6 jit_solution(3298601621659588823)
XLA Ops:
  0.6 0.0 copy-start
  0.7 0.0 copy-start.5
  0.7 0.0 copy-start.4
  0.7 30.4 %front.1 = (bf16[32,256,128]{2,1,0:T(8,128)(2,1)S(1)}, bf16[32,256,128]{2,1,0:T(8,128)(2,1)S(1)}, bf16[16,80,128]{2,1,0:T(8,128)(2,1)S(1)}, bf16[2,16,80,128]{3,...) custom-call(bf16[256,128]{1,0:T(8,128)(2,1)} %bitcast.35, ...), custom_call_target="tpu_custom_call" | custom-call | flops 1073741824 | bytes 16777216 | tf_op jit(solution)/shard_map/front/pallas_call | solution.py:546
  31.1 0.0 copy-done
  31.1 0.0 copy-done.5
  31.1 0.0 copy-done.4
  31.1 0.0 copy-start.1
  31.1 0.0 copy-start.2
  31.1 0.0 copy-start.3
  31.1 10.0 %attention.1 = (f32[256,1024]{1,0:T(8,128)S(1)}, bf16[256,1024]{1,0:T(8,128)(2,1)}, bf16[2,4,4,256,128]{4,3,2,1,0:T(8,128)(2,1)S(1)}, bf16[2,4,4,256,128]{4,3,2,1,0:T(8,128)(2,1)S(1)}) custom-call(s32[64,64]{1,0:T(8,128)S(1)} %bitcast.30, bf16[256,1024]{1,0:T(8,128)(2,1)S(1)} %bitcast.29, bf16[256,1024]{1,0:T(8,128)(2,1)S(1)} %bitcast.21, ...), custom_call_target="tpu_custom_call" | custom-call | flops 9663676416 | bytes 12582912 | tf_op jit(solution)/shard_map/attention/pallas_call | solution.py:150
  41.1 0.0 copy-done.1
  41.1 0.0 copy-done.2
  41.1 0.0 copy-done.3
  41.1 49.7 %back.1 = (bf16[256,128]{1,0:T(8,128)(2,1)S(1)}, bf16[256,128]{1,0:T(8,128)(2,1)S(1)}, bf16[256,1024]{1,0:T(8,128)(2,1)S(1)}, bf16[256,1024]{1,0:T(8,128)(2,1)S(...) custom-call(bf16[2,4,4,256,128]{4,3,2,1,0:T(8,128)(2,1)S(1)} %get-tuple-element.41.tk_ref, ...), custom_call_target="tpu_custom_call" | custom-call | flops 536870912 | bytes 16777216 | tf_op jit(solution)/shard_map/back/pallas_call | solution.py:858
  90.8 1.1 %emit.1 = (bf16[256,1024]{1,0:T(8,128)(2,1)}, bf16[256,1024]{1,0:T(8,128)(2,1)}, bf16[256,128]{1,0:T(8,128)(2,1)}, bf16[256,128]{1,0:T(8,128)(2,1)}, bf16[256,12...) custom-call(bf16[256,1024]{1,0:T(8,128)(2,1)S(1)} %get-tuple-element.54.refs_0_, ...), custom_call_target="tpu_custom_call" | custom-call | bytes 3145728 | tf_op jit(solution)/shard_map/emit/pallas_call | solution.py:906
  91.9 0.7 multiply_reduce_fusion
Async XLA Ops:
  0.6 30.4 %copy-start = (bf16[1,256,1024]{2,1,0:T(8,128)(2,1)S(1)}, bf16[1,256,1024]{2,1,0:T(8,128)(2,1)}, u32[]{:S(2)}) copy-start(bf16[1,256,1024]{2,1,0:T(8,128)(2,1)} %param.21) | copy-start | bytes 1572868
  0.7 30.4 %copy-start.5 = (s32[1,64,64]{2,1,0:T(8,128)S(1)}, s32[1,64,64]{2,1,0:T(8,128)}, u32[]{:S(2)}) copy-start(s32[1,64,64]{2,1,0:T(8,128)} %param.20) | copy-start | bytes 49156
  0.7 30.4 %copy-start.4 = (bf16[1,256,1024]{2,1,0:T(8,128)(2,1)S(1)}, bf16[1,256,1024]{2,1,0:T(8,128)(2,1)}, u32[]{:S(2)}) copy-start(bf16[1,256,1024]{2,1,0:T(8,128)(2,1)} %param.11) | copy-start | bytes 1572868
  31.1 10.0 %copy-start.1 = (bf16[1,256,1024]{2,1,0:T(8,128)(2,1)S(1)}, bf16[1,256,1024]{2,1,0:T(8,128)(2,1)}, u32[]{:S(2)}) copy-start(bf16[1,256,1024]{2,1,0:T(8,128)(2,1)} %param.14) | copy-start | bytes 1572868
  31.1 10.0 %copy-start.2 = (bf16[1,256,128]{2,1,0:T(8,128)(2,1)S(1)}, bf16[1,256,128]{2,1,0:T(8,128)(2,1)}, u32[]{:S(2)}) copy-start(bf16[1,256,128]{2,1,0:T(8,128)(2,1)} %param.15) | copy-start | bytes 196612
  31.1 10.0 %copy-start.3 = (bf16[1,256,128]{2,1,0:T(8,128)(2,1)S(1)}, bf16[1,256,128]{2,1,0:T(8,128)(2,1)}, u32[]{:S(2)}) copy-start(bf16[1,256,128]{2,1,0:T(8,128)(2,1)} %param.16) | copy-start | bytes 196612

commit v4 on v3

--- a/solution.py
+++ b/solution.py
@@ -131,7 +131,7 @@
         for h in range(HEADS):
             dq_ref[rows, cols(h)] = (dq_t[:, cols(h)] * FACTOR).T.astype(BF)
 
-    @pl.loop(0, total_blocks)
+    @pl.loop(0, total_blocks, unroll=4)
     def _(j):
         here = pl.ds(pl.multiple_of(j * BT, BT), BT)
         chip = j // 4
@@ -196,7 +196,7 @@
     return lax.rem(a + step + SIDE, SIDE)
 
 
-def greet(chip, core, also_dp):
+def greet(chip, core, also_dp, between=None):
     barrier = pltpu.get_barrier_semaphore()
 
     @pl.loop(1, CHIPS)
@@ -217,6 +217,8 @@
             pl.semaphore_signal(barrier, inc=1, device_id={"dp": to}, device_id_type=MESH)
 
         waits += LAYERS - 1
+    if between is not None:
+        between()
     pl.semaphore_wait(barrier, waits)
 
 
@@ -769,7 +771,12 @@
     me, x, y, core = place()
     layer = lax.axis_index("dp")
     chip = me // 2
-    greet(chip, core, True)
+
+    def local_scan():
+        sums_ref[...] = sums_in[...]
+        scan_states(me, got_ref, back_ref, kept, decays, logs, sums_ref)
+
+    greet(chip, core, True, local_scan)
     copies = Copies(send_sem, recv_sem)
 
     def dev_k(df, ds, other=False):
@@ -790,8 +797,6 @@
             getattr(part, name)()
 
     stage("begin")
-    sums_ref[...] = sums_in[...]
-    scan_states(me, got_ref, back_ref, kept, decays, logs, sums_ref)
     start, wait_states = to_peers(
         chip, core, lambda to: back_ref.at[to], st_ref.at[core, chip], s1, r1
     )
@@ -887,28 +892,35 @@
     )(tk, tv, got, sib, o, y, dx, xt, eg, db, dc, cum, sums, b, c, x, g)
 
 
-def emit_kernel(*refs):
-    count = (len(refs) - 2) // 2
-    total_ref, rate_ref = refs[count], refs[2 * count + 1]
+def emit_kernel(tokens, *refs):
+    count = (len(refs) - 4) // 2
+    total_ref, rate_ref, skip_ref = refs[count], refs[2 * count + 1], refs[2 * count + 2]
     sem = refs[-1]
     moves = [
         pltpu.make_async_copy(refs[i], refs[count + 1 + i], sem.at[i]) for i in range(count)
     ]
     for move in moves:
         move.start()
-    rate_ref[...] = total_ref[...]
+    diagonal = lax.broadcasted_iota(jnp.int32, (HEADS, HW), 0) == lax.broadcasted_iota(
+        jnp.int32, (HEADS, HW), 1
+    )
+    for ref, first, scale in ((rate_ref, 0, tokens), (skip_ref, HEADS, tokens * HW)):
+        picked = jnp.where(diagonal, total_ref[first : first + HEADS, :], 0.0)
+        row = jnp.sum(picked, axis=0, keepdims=True) / scale
+        ref[...] = row[:, :HEADS]
     for move in moves:
         move.wait()
 
 
-def emit(arrays, total):
+def emit(arrays, total, tokens):
     count = len(arrays)
+    small = jax.ShapeDtypeStruct((1, HEADS), F32)
     return pl.pallas_call(
-        emit_kernel,
+        functools.partial(emit_kernel, tokens),
         out_shape=tuple(pltpu.HBM(a.shape, a.dtype) for a in arrays)
-        + (jax.ShapeDtypeStruct(total.shape, total.dtype),),
+        + (small, small),
         in_specs=[VM] * (count + 1),
-        out_specs=(HB,) * count + (VM,),
+        out_specs=(HB,) * count + (VM, VM),
         scratch_shapes=[pltpu.SemaphoreType.DMA((count,))],
         compiler_params=pltpu.CompilerParams(vmem_limit_bytes=4 << 20),
         cost_estimate=pl.CostEstimate(flops=0, bytes_accessed=3 << 20, transcendentals=0),
@@ -928,8 +940,10 @@
     dk, dv, layer_out, dx, db, dc, total = back(
         terms_k, terms_v, got, sib, attended, *local_terms, b, c, x, g
     )
-    layer_out, dx, dk, dv, db, dc, total = emit((layer_out, dx, dk, dv, db, dc), total)
     tokens = lax.axis_size("dp") * lax.axis_size("seq") * local
+    layer_out, dx, dk, dv, db, dc, rate, gain = emit(
+        (layer_out, dx, dk, dv, db, dc), total, tokens
+    )
     return (
         layer_out[None],
         dq[None],
@@ -938,8 +952,8 @@
         dx[None],
         db[None],
         dc[None],
-        total[:HEADS, 0] / tokens,
-        total[HEADS:, 0] / (tokens * HW),
+        rate[0],
+        gain[0],
     )
 
 

time: 94 us -> 93.8 us (level)
  no operation moved by 1% of the time
where the time goes in v4:
time: 93.8 us; the launch traced here: 92.3 us
  Pallas kernels  91.3 us (97%)
    pallas_call x1, Pallas kernels, back(): pl.pallas_call(back_kernel, out_shape=(small, small, sds((local, wide), B...  49.8 us
    pallas_call x1, Pallas kernels, front(): pl.pallas_call(front_kernel, out_shape=(full, full, sds((CHIPS, PACKED, H...  30.4 us
    pallas_call x1, Pallas kernels, attention(): pl.pallas_call(attention_kernel, out_shape=(jax.ShapeDtypeStruct((local,...  9.58 us

profile of v4, /device:TPU:1, one launch (start us, length us, event | category | flops | bytes accessed | tf_op | source)
XLA Modules:
  0.0 92.3 jit_solution(17686772699592066172)
XLA Ops:
  0.6 0.0 copy-start
  0.7 0.0 copy-start.5
  0.7 0.0 copy-start.4
  0.7 30.4 %front.1 = (bf16[32,256,128]{2,1,0:T(8,128)(2,1)S(1)}, bf16[32,256,128]{2,1,0:T(8,128)(2,1)S(1)}, bf16[16,80,128]{2,1,0:T(8,128)(2,1)S(1)}, bf16[2,16,80,128]{3,...) custom-call(bf16[256,128]{1,0:T(8,128)(2,1)} %bitcast.37, ...), custom_call_target="tpu_custom_call" | custom-call | flops 1073741824 | bytes 16777216 | tf_op jit(solution)/shard_map/front/pallas_call | solution.py:548
  31.1 0.0 copy-done
  31.1 0.0 copy-done.5
  31.1 0.0 copy-done.4
  31.1 0.0 copy-start.1
  31.1 0.0 copy-start.2
  31.1 0.0 copy-start.3
  31.1 9.6 %attention.1 = (f32[256,1024]{1,0:T(8,128)S(1)}, bf16[256,1024]{1,0:T(8,128)(2,1)}, bf16[2,4,4,256,128]{4,3,2,1,0:T(8,128)(2,1)S(1)}, bf16[2,4,4,256,128]{4,3,2,1,0:T(8,128)(2,1)S(1)}) custom-call(s32[64,64]{1,0:T(8,128)S(1)} %bitcast.32, bf16[256,1024]{1,0:T(8,128)(2,1)S(1)} %bitcast.31, bf16[256,1024]{1,0:T(8,128)(2,1)S(1)} %bitcast.23, ...), custom_call_target="tpu_custom_call" | custom-call | flops 9663676416 | bytes 12582912 | tf_op jit(solution)/shard_map/attention/pallas_call | solution.py:150
  40.7 0.0 copy-done.1
  40.7 0.0 copy-done.2
  40.7 0.0 copy-done.3
  40.7 49.8 %back.1 = (bf16[256,128]{1,0:T(8,128)(2,1)S(1)}, bf16[256,128]{1,0:T(8,128)(2,1)S(1)}, bf16[256,1024]{1,0:T(8,128)(2,1)S(1)}, bf16[256,1024]{1,0:T(8,128)(2,1)S(...) custom-call(bf16[2,4,4,256,128]{4,3,2,1,0:T(8,128)(2,1)S(1)} %get-tuple-element.42.tk_ref, ...), custom_call_target="tpu_custom_call" | custom-call | flops 536870912 | bytes 16777216 | tf_op jit(solution)/shard_map/back/pallas_call | solution.py:863
  90.5 1.6 %emit.1 = (bf16[256,1024]{1,0:T(8,128)(2,1)}, bf16[256,1024]{1,0:T(8,128)(2,1)}, bf16[256,128]{1,0:T(8,128)(2,1)}, bf16[256,128]{1,0:T(8,128)(2,1)}, bf16[256,12...) custom-call(bf16[256,1024]{1,0:T(8,128)(2,1)S(1)} %get-tuple-element.55.refs_0_, ...), custom_call_target="tpu_custom_call" | custom-call | bytes 3145728 | tf_op jit(solution)/shard_map/emit/pallas_call | solution.py:918
Async XLA Ops:
  0.6 30.4 %copy-start = (bf16[1,256,1024]{2,1,0:T(8,128)(2,1)S(1)}, bf16[1,256,1024]{2,1,0:T(8,128)(2,1)}, u32[]{:S(2)}) copy-start(bf16[1,256,1024]{2,1,0:T(8,128)(2,1)} %param.21) | copy-start | bytes 1572868
  0.7 30.4 %copy-start.5 = (s32[1,64,64]{2,1,0:T(8,128)S(1)}, s32[1,64,64]{2,1,0:T(8,128)}, u32[]{:S(2)}) copy-start(s32[1,64,64]{2,1,0:T(8,128)} %param.20) | copy-start | bytes 49156
  0.7 30.4 %copy-start.4 = (bf16[1,256,1024]{2,1,0:T(8,128)(2,1)S(1)}, bf16[1,256,1024]{2,1,0:T(8,128)(2,1)}, u32[]{:S(2)}) copy-start(bf16[1,256,1024]{2,1,0:T(8,128)(2,1)} %param.11) | copy-start | bytes 1572868
  31.1 9.6 %copy-start.1 = (bf16[1,256,1024]{2,1,0:T(8,128)(2,1)S(1)}, bf16[1,256,1024]{2,1,0:T(8,128)(2,1)}, u32[]{:S(2)}) copy-start(bf16[1,256,1024]{2,1,0:T(8,128)(2,1)} %param.14) | copy-start | bytes 1572868
  31.1 9.6 %copy-start.2 = (bf16[1,256,128]{2,1,0:T(8,128)(2,1)S(1)}, bf16[1,256,128]{2,1,0:T(8,128)(2,1)}, u32[]{:S(2)}) copy-start(bf16[1,256,128]{2,1,0:T(8,128)(2,1)} %param.15) | copy-start | bytes 196612
  31.1 9.6 %copy-start.3 = (bf16[1,256,128]{2,1,0:T(8,128)(2,1)S(1)}, bf16[1,256,128]{2,1,0:T(8,128)(2,1)}, u32[]{:S(2)}) copy-start(bf16[1,256,128]{2,1,0:T(8,128)(2,1)} %param.16) | copy-start | bytes 196612

commit v5 on v4

--- a/solution.py
+++ b/solution.py
@@ -804,10 +804,10 @@
     start()
     st_ref[core, chip] = back_ref[chip]
     stage("two")
+    stage("three")
     wait_states()
     pair = to_sibling(chip, core, st_ref.at[core], st_ref.at[core], pair_sem)
     pair.start()
-    stage("three")
     pair.wait()
     ssm_finish(
         core, st_ref, sib_ref, o_ref, y_ref, dx_ref, xt_ref, eg_ref, db_ref, dc_ref, cum_ref,

time: 93.8 us -> 95.4 us (1.017); the launches traced: 92.3 us -> 95.6 us
  Pallas kernels: 91.3 us -> 94.7 us
    pallas_call x1, Pallas kernels: 49.8 us -> 53.1 us  [back(): pl.pallas_call(back_kernel, out_shape=(small, small, sds((local, wide), B...]
where the time goes in v5:
time: 95.4 us; the launch traced here: 95.6 us
  Pallas kernels  94.7 us (99%)
    pallas_call x1, Pallas kernels, back(): pl.pallas_call(back_kernel, out_shape=(small, small, sds((local, wide), B...  53.1 us
    pallas_call x1, Pallas kernels, front(): pl.pallas_call(front_kernel, out_shape=(full, full, sds((CHIPS, PACKED, H...  30.4 us
    pallas_call x1, Pallas kernels, attention(): pl.pallas_call(attention_kernel, out_shape=(jax.ShapeDtypeStruct((local,...  9.58 us

profile of v5, /device:TPU:1, one launch (start us, length us, event | category | flops | bytes accessed | tf_op | source)
XLA Modules:
  0.0 95.6 jit_solution(4368538697426212245)
XLA Ops:
  0.6 0.0 copy-start
  0.7 0.0 copy-start.5
  0.7 0.0 copy-start.4
  0.7 30.4 %front.1 = (bf16[32,256,128]{2,1,0:T(8,128)(2,1)S(1)}, bf16[32,256,128]{2,1,0:T(8,128)(2,1)S(1)}, bf16[16,80,128]{2,1,0:T(8,128)(2,1)S(1)}, bf16[2,16,80,128]{3,...) custom-call(bf16[256,128]{1,0:T(8,128)(2,1)} %bitcast.37, ...), custom_call_target="tpu_custom_call" | custom-call | flops 1073741824 | bytes 16777216 | tf_op jit(solution)/shard_map/front/pallas_call | solution.py:548
  31.1 0.0 copy-done
  31.1 0.0 copy-done.5
  31.1 0.0 copy-done.4
  31.1 0.0 copy-start.1
  31.1 0.0 copy-start.2
  31.1 0.0 copy-start.3
  31.1 9.6 %attention.1 = (f32[256,1024]{1,0:T(8,128)S(1)}, bf16[256,1024]{1,0:T(8,128)(2,1)}, bf16[2,4,4,256,128]{4,3,2,1,0:T(8,128)(2,1)S(1)}, bf16[2,4,4,256,128]{4,3,2,1,0:T(8,128)(2,1)S(1)}) custom-call(s32[64,64]{1,0:T(8,128)S(1)} %bitcast.32, bf16[256,1024]{1,0:T(8,128)(2,1)S(1)} %bitcast.31, bf16[256,1024]{1,0:T(8,128)(2,1)S(1)} %bitcast.23, ...), custom_call_target="tpu_custom_call" | custom-call | flops 9663676416 | bytes 12582912 | tf_op jit(solution)/shard_map/attention/pallas_call | solution.py:150
  40.7 0.0 copy-done.1
  40.7 0.0 copy-done.2
  40.7 0.0 copy-done.3
  40.7 53.1 %back.1 = (bf16[256,128]{1,0:T(8,128)(2,1)S(1)}, bf16[256,128]{1,0:T(8,128)(2,1)S(1)}, bf16[256,1024]{1,0:T(8,128)(2,1)S(1)}, bf16[256,1024]{1,0:T(8,128)(2,1)S(...) custom-call(bf16[2,4,4,256,128]{4,3,2,1,0:T(8,128)(2,1)S(1)} %get-tuple-element.42.tk_ref, ...), custom_call_target="tpu_custom_call" | custom-call | flops 536870912 | bytes 16777216 | tf_op jit(solution)/shard_map/back/pallas_call | solution.py:863
  93.8 1.6 %emit.1 = (bf16[256,1024]{1,0:T(8,128)(2,1)}, bf16[256,1024]{1,0:T(8,128)(2,1)}, bf16[256,128]{1,0:T(8,128)(2,1)}, bf16[256,128]{1,0:T(8,128)(2,1)}, bf16[256,12...) custom-call(bf16[256,1024]{1,0:T(8,128)(2,1)S(1)} %get-tuple-element.55.refs_0_, ...), custom_call_target="tpu_custom_call" | custom-call | bytes 3145728 | tf_op jit(solution)/shard_map/emit/pallas_call | solution.py:918
Async XLA Ops:
  0.6 30.4 %copy-start = (bf16[1,256,1024]{2,1,0:T(8,128)(2,1)S(1)}, bf16[1,256,1024]{2,1,0:T(8,128)(2,1)}, u32[]{:S(2)}) copy-start(bf16[1,256,1024]{2,1,0:T(8,128)(2,1)} %param.21) | copy-start | bytes 1572868
  0.7 30.4 %copy-start.5 = (s32[1,64,64]{2,1,0:T(8,128)S(1)}, s32[1,64,64]{2,1,0:T(8,128)}, u32[]{:S(2)}) copy-start(s32[1,64,64]{2,1,0:T(8,128)} %param.20) | copy-start | bytes 49156
  0.7 30.4 %copy-start.4 = (bf16[1,256,1024]{2,1,0:T(8,128)(2,1)S(1)}, bf16[1,256,1024]{2,1,0:T(8,128)(2,1)}, u32[]{:S(2)}) copy-start(bf16[1,256,1024]{2,1,0:T(8,128)(2,1)} %param.11) | copy-start | bytes 1572868
  31.1 9.6 %copy-start.1 = (bf16[1,256,1024]{2,1,0:T(8,128)(2,1)S(1)}, bf16[1,256,1024]{2,1,0:T(8,128)(2,1)}, u32[]{:S(2)}) copy-start(bf16[1,256,1024]{2,1,0:T(8,128)(2,1)} %param.14) | copy-start | bytes 1572868
  31.1 9.6 %copy-start.2 = (bf16[1,256,128]{2,1,0:T(8,128)(2,1)S(1)}, bf16[1,256,128]{2,1,0:T(8,128)(2,1)}, u32[]{:S(2)}) copy-start(bf16[1,256,128]{2,1,0:T(8,128)(2,1)} %param.15) | copy-start | bytes 196612
  31.1 9.6 %copy-start.3 = (bf16[1,256,128]{2,1,0:T(8,128)(2,1)S(1)}, bf16[1,256,128]{2,1,0:T(8,128)(2,1)}, u32[]{:S(2)}) copy-start(bf16[1,256,128]{2,1,0:T(8,128)(2,1)} %param.16) | copy-start | bytes 196612
